TPU v7x, 128 devices: a whole 4x4x4 slice. The times are simulated.
128 devices in a mesh: param: 4 (over z_lo, core), space: 32 (over y, z_hi, x).
Axes of the slice: x: 4, y: 4, z: 4 (z_hi: 2, z_lo: 2; z = z_hi * 2 + z_lo), core: 2. Of those that a mesh axis runs over, the one named last changes fastest.
Arguments:
- fine_state: bfloat16 [64, 16, 64, 512], P('space', None, None, 'param'), may hold values from -6 to 6
- fine_tangent: bfloat16 [64, 16, 64, 512], P('space', None, None, 'param'), may hold values from -6 to 6
- down_weight: float32 [8, 512, 1024], P(None, 'space', 'param'), may hold values from -0.09375 to 0.09375
- conv_weight: float32 [27, 1024, 1024], P(None, 'space', 'param'), may hold values from -0.0390625 to 0.0390625
- up_weight: float32 [8, 1024, 512], P(None, 'space', 'param'), may hold values from -0.1875 to 0.1875
Outputs:
- state_out: bfloat16 [64, 16, 64, 512], P('space', None, None, 'param')
- tangent_out: bfloat16 [64, 16, 64, 512], P('space', None, None, 'param')
All inputs are finite; a program needn't handle non-finite values.
Results may differ from a plain program's by a relative error of at most 0.0075.
Values may be sent and summed in bfloat16 or wider, within the bound.
A program may use at most 128 MiB of HBM per device.

v0:
```python
import jax
import jax.numpy as jnp
from jax import lax
from jax.sharding import PartitionSpec as P


def padded_2(block, sides, width):
    for axis, dim in sides:
        count = lax.axis_size(axis)
        forward = [(i, i + 1) for i in range(count - 1)]
        backward = [(target, source) for source, target in forward]
        low = lax.ppermute(
            lax.slice_in_dim(block, block.shape[dim] - width, None, axis=dim), axis, forward
        )
        high = lax.ppermute(lax.slice_in_dim(block, 0, width, axis=dim), axis, backward)
        block = jnp.concatenate([low, block, high], axis=dim)
    return block


def silu_pair(primal, tangent):
    sigma = jax.nn.sigmoid(primal)
    return (primal * sigma, sigma * (1.0 + primal * (1.0 - sigma)) * tangent)


def cube_block(source, kernel, planes):
    span_y = source.shape[2] - 2
    span_x = source.shape[3] - 2
    width = source.shape[4]
    result = None
    for tap_z in range(3):
        for tap_y in range(3):
            window = jnp.stack(
                [
                    source[
                        :, tap_z : tap_z + planes, tap_y : tap_y + span_y, tap_x : tap_x + span_x, :
                    ]
                    for tap_x in range(3)
                ],
                axis=4,
            )
            window = window.reshape(-1, 3 * width)
            first_tap = 9 * tap_z + 3 * tap_y
            weights = kernel[first_tap : first_tap + 3].reshape(3 * width, kernel.shape[2])
            term = jnp.dot(window, weights, preferred_element_type=jnp.float32)
            result = term if result is None else result + term
    return result


def local(fine_state, fine_tangent, down_weight, conv_weight, up_weight):
    planes = fine_state.shape[0] // 2
    span_y = fine_state.shape[1] // 2
    span_x = fine_state.shape[2] // 2
    cells = planes * span_y * span_x
    state_full, tangent_full = (
        lax.all_gather(fine_state, "param", axis=3, tiled=True),
        lax.all_gather(fine_tangent, "param", axis=3, tiled=True),
    )
    wide_fine = state_full.shape[3]
    paired = jnp.stack([state_full, tangent_full], axis=0)
    patches = (
        paired.reshape(2, planes, 2, span_y, 2, span_x, 2, wide_fine)
        .transpose(0, 1, 3, 5, 2, 4, 6, 7)
        .reshape(2 * cells, 8, wide_fine)
    )
    down_kernel = down_weight.astype(jnp.bfloat16)
    up_kernel = up_weight.astype(jnp.bfloat16)
    cube_kernel = conv_weight.astype(jnp.bfloat16)
    coarse_local = down_weight.shape[2]
    fine_local = up_weight.shape[2]
    portion = lax.all_gather(down_kernel, "space", axis=1, tiled=True)
    width = portion.shape[1]
    columns = patches.reshape(2 * cells, 8 * width)
    first_pre = jnp.dot(
        columns, portion.reshape(8 * width, portion.shape[2]), preferred_element_type=jnp.float32
    )
    first_pre = first_pre.reshape(2, cells, coarse_local)
    first_val, first_dir = silu_pair(first_pre[0], first_pre[1])
    first_round = jnp.stack(
        [first_val.astype(jnp.bfloat16), first_dir.astype(jnp.bfloat16)], axis=0
    )
    first_stack = first_round.reshape(2, planes, span_y, span_x, coarse_local)
    haloed = padded_2(first_stack, (("space", 1),), 1)
    every_channel = lax.all_gather(haloed, "param", axis=4, tiled=True)
    padded = jnp.pad(every_channel, ((0, 0), (0, 0), (1, 1), (1, 1), (0, 0)))
    second_pre = cube_block(
        padded, lax.all_gather(cube_kernel, "space", axis=1, tiled=True), planes
    ).reshape(2, cells, coarse_local)
    second_val, second_dir = silu_pair(second_pre[0], second_pre[1])
    second_val = second_val + first_round[0].astype(jnp.float32)
    second_dir = second_dir + first_round[1].astype(jnp.float32)
    top_stack = jnp.stack(
        [second_val.astype(jnp.bfloat16), second_dir.astype(jnp.bfloat16)], axis=0
    )
    top_full = lax.all_gather(top_stack, "param", axis=2, tiled=True)
    top_rows = top_full.reshape(2 * cells, top_full.shape[2])
    portion = lax.all_gather(up_kernel, "space", axis=1, tiled=True)
    width = portion.shape[1]
    columns = top_rows
    product = jnp.dot(
        columns,
        portion.transpose(1, 0, 2).reshape(width, 8 * fine_local),
        preferred_element_type=jnp.float32,
    )
    shaped = product.reshape(2, planes, span_y, span_x, 2, 2, 2, fine_local).transpose(
        0, 1, 4, 2, 5, 3, 6, 7
    )
    outputs = shaped.reshape(2, 2 * planes, 2 * span_y, 2 * span_x, fine_local).astype(jnp.bfloat16)
    return (outputs[0], outputs[1])


def solution(mesh):
    in_specs = (
        P("space", None, None, "param"),
        P("space", None, None, "param"),
        P(None, "space", "param"),
        P(None, "space", "param"),
        P(None, "space", "param"),
    )
    out_specs = (P("space", None, None, "param"), P("space", None, None, "param"))
    return jax.shard_map(local, mesh=mesh, in_specs=in_specs, out_specs=out_specs, check_vma=False)
```

profile of v0, /device:TPU:5, one launch (start us, length us, event | category | flops | bytes accessed | tf_op | source)
XLA Modules:
  0.0 463.3 jit_solution(5521071083884901412)
XLA Ops:
  7.2 0.7 all-gather.8.cloned.1.call-update
  7.9 0.7 all-gather.10.cloned.1.call-update
  8.7 1.5 convert_element_type.39
  10.3 31.2 %all-gather.8.cloned.1.call-done = bf16[2,16,64,512]{3,2,1,0:T(8,128)(2,1)} async-done(((bf16[2,16,64,128]{3,2,1,0:T(8,128)(2,1)}), bf16[2,16,64,512]{3,2,1,0:T(8,128)(2,1)}) %all-gather.8.cloned.1.call-update) | async-done | bytes 2097168 | tf_op jit(solution)/shard_map/all_gather | solution.py:55
  41.5 2.7 stack.135
  44.3 28.9 %all-gather.10.cloned.1.call-done = bf16[2,16,64,512]{3,2,1,0:T(8,128)(2,1)} async-done(((bf16[2,16,64,128]{3,2,1,0:T(8,128)(2,1)}), bf16[2,16,64,512]{3,2,1,0:T(8,128)(2,1)}) %all-gather.10.cloned.1.call-update) | async-done | bytes 2097168 | tf_op jit(solution)/shard_map/all_gather | solution.py:56
  73.1 4.1 stack.136
  77.3 7.8 %copy_bitcast_fusion = bf16[2,1,8,32,2,2,2,512]{7,6,5,4,3,2,0,1:T(2,128)(2,1)} fusion(bf16[1,1,2,8,2,32,2,512]{7,6,5,4,3,2,1,0:T(2,128)(2,1)} %stack.136, bf16[1,1,2,8,2,32,2,512]{7,6,5,4,3,2,1,0:T(2,128)(2,1)S(1)} %stack.135), kind=kLoop, calls=%fused_computation.25 | loop fusion | flops 2097152 | bytes 8388608 | tf_op jit(solution)/shard_map/transpose | solution.py:62
  85.1 7.9 %reshape_reshape.3 = bf16[512,4096]{1,0:T(8,128)(2,1)} reshape(bf16[2,1,8,32,2,2,2,512]{7,6,5,4,3,2,0,1:T(2,128)(2,1)} %copy_bitcast_fusion) | data formatting | bytes 8388608 | tf_op jit(solution)/shard_map/reshape;reshape | solution.py:72
  92.9 55.3 %all-gather.12.cloned.1.call-done = bf16[8,512,256]{2,1,0:T(8,128)(2,1)} async-done(((bf16[8,16,256]{2,1,0:T(8,128)(2,1)}), bf16[8,512,256]{2,1,0:T(8,128)(2,1)}) %all-gather.12.cloned.1.call-update) | async-done | bytes 2097168 | tf_op jit(solution)/shard_map/all_gather | solution.py:70
  148.2 4.1 fusion.32
  152.5 2.6 collective-permute-start.1
  155.2 2.8 collective-permute-start
  158.0 2.5 collective-permute-done.1
  160.5 2.2 collective-permute-done
  162.7 1.0 pad_maximum_fusion.10
  163.7 0.8 convert_element_type.42
  164.7 0.7 copy.74
  165.4 42.8 %all-gather.14.cloned.1.call-done = bf16[2,3,8,32,1024]{4,3,2,0,1:T(8,128)(2,1)} async-done(((bf16[2,3,8,32,256]{4,3,2,0,1:T(8,128)(2,1)}), bf16[2,3,8,32,1024]{4,3,2,0,1:T(8,128)(2,1)}) %all-gather.14.cloned.1.call-update) | async-done | bytes 3145744 | tf_op jit(solution)/shard_map/all_gather | solution.py:83
  208.2 5.3 %fusion.23 = (bf16[2,1,8,32,1,1024]{5,3,2,0,4,1:T(8,128)(2,1)S(1)}, bf16[2,1,8,32,1,1024]{5,3,2,0,4,1:T(8,128)(2,1)S(1)}, bf16[2,1,8,32,1,1024]{5,3,2,0,4,1:T(8,...) fusion(bf16[2,3,8,32,1024]{4,3,2,0,1:T(8,128)(2,1)} %all-gather, ...), kind=kLoop, calls=%fused_computation.67 | loop fusion | bytes 14680064 | tf_op jit(solution)/shard_map/stack | solution.py:32
  213.9 2.7 copy.54
  216.6 3.4 copy.70
  220.1 7.1 %fusion.22 = (bf16[2,1,8,32,1,1024]{5,3,2,0,4,1:T(8,128)(2,1)}, bf16[2,1,8,32,1,1024]{5,3,2,0,4,1:T(8,128)(2,1)}, bf16[2,1,8,32,1,1024]{5,3,2,0,4,1:T(8,128)(2,1...) fusion(bf16[2,3,8,32,1024]{4,3,2,0,1:T(8,128)(2,1)S(1)} %copy-done), kind=kLoop, calls=%fused_computation.66 | loop fusion | bytes 23068672 | tf_op jit(solution)/shard_map/stack | solution.py:32
  227.2 2.7 pad_maximum_fusion.7
  229.9 2.7 copy.53
  232.7 3.4 copy.69
  236.1 2.7 copy.55
  238.9 3.4 copy.71
  242.3 1.1 pad_maximum_fusion.1
  243.5 2.7 copy.47
  246.2 3.5 copy.63
  249.7 2.7 copy.48
  252.5 3.6 copy.64
  256.1 0.9 pad_maximum_fusion.5
  257.0 2.7 copy.51
  259.8 3.4 copy.67
  263.1 2.7 copy.52
  265.9 3.4 copy.68
  269.4 0.9 pad_maximum_fusion.3
  270.3 2.7 copy.49
  273.1 3.4 copy.65
  276.5 2.7 copy.50
  279.2 3.4 copy.66
  282.6 73.8 %all-gather.16.cloned.1.call-done = bf16[27,1024,256]{2,1,0:T(8,128)(2,1)} async-done(((bf16[27,32,256]{2,1,0:T(8,128)(2,1)}), bf16[27,1024,256]{2,1,0:T(8,128)(2,1)}) %all-gather.16.cloned.1.call-update) | async-done | bytes 14155792 | tf_op jit(solution)/shard_map/all_gather | solution.py:86
  356.4 6.2 %fusion.30 = (bf16[3,1024,256]{2,1,0:T(8,128)(2,1)S(1)}, bf16[3,1024,256]{2,1,0:T(8,128)(2,1)S(1)}, bf16[3,1024,256]{2,1,0:T(8,128)(2,1)S(1)}, bf16[3,1024,256]{...) fusion(bf16[27,1024,256]{2,1,0:T(8,128)(2,1)} %all-gather.16.cl, ...), kind=kLoop, calls=%fused_computation.87 | loop fusion | bytes 28311552 | tf_op jit(solution)/shard_map/slice | solution.py:43
  362.7 1.0 fusion.33
  363.7 0.9 copy-done.18
  364.6 1.0 convolution_add_fusion.7
  365.8 1.0 convolution_add_fusion.6
  366.8 0.7 copy-done.22
  367.5 1.0 convolution_add_fusion.5
  368.9 1.0 convolution_add_fusion.4
  369.9 0.6 copy-done.20
  370.5 1.0 convolution_add_fusion.3
  371.9 1.0 convolution_add_fusion.2
  373.5 1.0 convolution_add_fusion.1
  375.0 1.0 convolution_add_fusion
  376.2 0.7 pad_maximum_fusion.12
  376.9 50.5 %all-gather.20.cloned.1.call-done = bf16[8,1024,128]{2,0,1:T(8,128)(2,1)} async-done(((bf16[8,32,128]{2,0,1:T(8,128)(2,1)}), bf16[8,1024,128]{2,0,1:T(8,128)(2,1)}) %all-gather.20.cloned.1.call-update) | async-done | bytes 2097168 | tf_op jit(solution)/shard_map/all_gather | solution.py:96
  427.4 3.2 copy.57
  430.6 20.1 %all-gather.18.cloned.1.call-done = bf16[2,256,1024]{2,1,0:T(8,128)(2,1)} async-done(((bf16[2,256,256]{2,1,0:T(8,128)(2,1)}), bf16[2,256,1024]{2,1,0:T(8,128)(2,1)}) %all-gather.18.cloned.1.call-update) | async-done | bytes 1048592 | tf_op jit(solution)/shard_map/all_gather | solution.py:94
  450.7 2.5 fusion
  453.3 1.3 copy.59
  454.7 1.3 copy.58
  (64 shorter events, 3.2 us)
Async XLA Ops:
  7.2 34.4 %all-gather.8.cloned.1.call-start = ((), (), s32[]{:S(2)}) async-start(), calls=%async_computation | async-start | bytes 2621440 | tf_op jit(solution)/shard_map/all_gather | solution.py:55
  7.9 65.2 %all-gather.10.cloned.1.call-start = ((), (), s32[]{:S(2)}) async-start(), calls=%async_computation.1 | async-start | bytes 2621440 | tf_op jit(solution)/shard_map/all_gather | solution.py:56
  8.6 139.6 %all-gather.12.cloned.1.call-start = ((), (), s32[]{:S(2)}) async-start(), calls=%async_computation.2 | async-start | bytes 2162688 | tf_op jit(solution)/shard_map/all_gather | solution.py:70
  10.3 198.0 %all-gather.14.cloned.1.call-start = ((), (), s32[]{:S(2)}) async-start(), calls=%async_computation.3 | async-start | bytes 3932160 | tf_op jit(solution)/shard_map/all_gather | solution.py:83
  152.4 11.4 %copy-start.23 = (f32[27,32,256]{2,1,0:T(8,128)S(1)}, f32[27,32,256]{2,1,0:T(8,128)}, u32[]{:S(2)}) copy-start(f32[27,32,256]{2,1,0:T(8,128)} %param.8) | copy-start | bytes 2654212
  152.4 12.3 %copy-start.24 = (f32[8,32,128]{2,1,0:T(8,128)S(1)}, f32[8,32,128]{2,1,0:T(8,128)}, u32[]{:S(2)}) copy-start(f32[8,32,128]{2,1,0:T(8,128)} %param.9) | copy-start | bytes 393220
  152.5 7.9 %collective-permute-start.1 = (bf16[2,1,8,32,256]{4,3,2,0,1:T(8,128)(2,1)S(1)}, bf16[2,1,8,32,256]{4,3,2,0,1:T(8,128)(2,1)S(1)}, u32[]{:S(2)}, u32[]{:S(2)}) collective-permute-start(bf16[2,1,8,32,256]{4,3,2,0,1:T(8,128)(2,1)S(1)} %pad_maximum_fusion.11), channel_id=1, source_target_pairs={{1,0},{2,1},{3,2},{4,3},{5,4},{6,5},{7,6},{8,7},{9,8},{10,9},{11,1... | collective-permute-start | bytes 786440 | tf_op jit(solution)/shard_map/ppermute | solution.py:15
  155.2 7.5 %collective-permute-start = (bf16[2,1,8,32,256]{4,3,2,0,1:T(8,128)(2,1)S(1)}, bf16[2,1,8,32,256]{4,3,2,0,1:T(8,128)(2,1)S(1)}, u32[]{:S(2)}, u32[]{:S(2)}) collective-permute-start(bf16[2,1,8,32,256]{4,3,2,0,1:T(8,128)(2,1)S(1)} %pad_maximum_fusion.11), channel_id=1, source_target_pairs={{0,1},{1,2},{2,3},{3,4},{4,5},{5,6},{6,7},{7,8},{8,9},{9,10},{10,1... | collective-permute-start | bytes 786440 | tf_op jit(solution)/shard_map/ppermute | solution.py:12
  163.7 192.7 %all-gather.16.cloned.1.call-start = ((), (), s32[]{:S(2)}) async-start(), calls=%async_computation.4 | async-start | bytes 14598144 | tf_op jit(solution)/shard_map/all_gather | solution.py:86
  164.6 262.8 %all-gather.20.cloned.1.call-start = ((), (), s32[]{:S(2)}) async-start(), calls=%async_computation.6 | async-start | bytes 2162688 | tf_op jit(solution)/shard_map/all_gather | solution.py:96
  165.4 285.3 %all-gather.18.cloned.1.call-start = ((), (), s32[]{:S(2)}) async-start(), calls=%async_computation.5 | async-start | bytes 1310720 | tf_op jit(solution)/shard_map/all_gather | solution.py:94
  216.6 3.4 copy-start
  238.8 3.5 copy-start.10
  238.9 3.5 copy-start.11
  238.9 3.5 copy-start.12
  238.9 3.4 copy-start.13
  252.4 3.6 copy-start.5
  252.5 3.6 copy-start.6
  252.5 3.6 copy-start.7
  252.5 3.6 copy-start.8
  252.5 3.6 copy-start.9
  265.9 3.5 copy-start.1
  265.9 3.5 copy-start.2
  265.9 3.5 copy-start.3
  265.9 3.5 copy-start.4
  282.6 80.1 %copy-start.17 = (bf16[64,8,3,1024]{3,1,2,0:T(8,128)(2,1)S(1)}, bf16[64,8,3,1024]{3,1,2,0:T(8,128)(2,1)}, u32[]{:S(2)}) copy-start(bf16[64,8,3,1024]{3,1,2,0:T(8,128)(2,1)} %copy.63) | copy-start | bytes 9437188
  362.7 1.9 copy-start.18
  363.7 2.1 copy-start.21
  365.6 1.9 copy-start.22
  366.8 2.1 copy-start.19
  368.5 2.0 copy-start.20
  369.9 2.1 copy-start.16
  371.5 2.0 copy-start.14
  373.0 2.0 copy-start.15
Sparse Core Ops, SparseCore 0:
  9.7 31.8 all-gather.7
  43.2 29.9 all-gather.9
  76.5 71.6 all-gather.11
  163.8 44.3 all-gather.13
  211.7 144.7 all-gather.15
  359.9 67.4 all-gather.19
  429.6 21.0 all-gather.17
where the time goes:
time: 473 us; the launch traced here: 463 us
  waiting for transfers between devices  309 us (65%)
  local copies, waits for them, and re-layouts  99.9 us (21%)
  other arithmetic  18.2 us (4%)
  matrix products  15.6 us (3%)
  between operations  15.1 us (3%)
  starting transfers between devices  5.7 us (1%)
    all_gather x1, waiting for transfers between devices, local(): lax.all_gather(cube_kernel, 'space', axis=1, tiled=True)  73.8 us
    all_gather x1, waiting for transfers between devices, local(): portion = lax.all_gather(down_kernel, 'space', axis=1, tiled=True)  55.3 us
    all_gather x1, waiting for transfers between devices, local(): portion = lax.all_gather(up_kernel, 'space', axis=1, tiled=True)  50.5 us
    all_gather x1, waiting for transfers between devices, local(): every_channel = lax.all_gather(haloed, 'param', axis=4, tiled=True)  42.8 us
    another operation x11, local copies, waits for them, and re-layouts, cube_block(): jnp.stack([source[:, tap_z:tap_z + planes, tap_y:tap_y + span_y, tap_x:ta...  37 us
    unnamed x60, local copies, waits for them, and re-layouts  35.9 us
    all_gather x1, waiting for transfers between devices, local(): lax.all_gather(fine_state, 'param', axis=3, tiled=True)  31.2 us
    all_gather x1, waiting for transfers between devices, local(): lax.all_gather(fine_tangent, 'param', axis=3, tiled=True)  28.9 us
  transfers between devices with their start and end apart: 9, of which 9 were waited for; matrix products, arithmetic and copies ran while one was open for 26% of the time, Pallas kernels for 0%

commit v1 on v0

v1 whole, which is shorter than its diff:
```python
import jax
import jax.numpy as jnp
from jax import lax
from jax.experimental import pallas as pl
from jax.experimental.pallas import tpu as pltpu
from jax.sharding import PartitionSpec as P

MESH = pl.DeviceIdType.MESH
F32 = jnp.float32
BF16 = jnp.bfloat16


def silu_pair(primal, tangent):
    sigma = jax.nn.sigmoid(primal)
    return primal * sigma, sigma * (1.0 + primal * (1.0 - sigma)) * tangent


class Links:
    def __init__(self, send_sems, recv_sems, count):
        self.send_sems, self.recv_sems, self.count = send_sems, recv_sems, count
        self.used = 0
        self.sent = []

    def copy(self, src, dst, device, slot=None):
        at = self.used
        self.used += 1
        assert self.used <= self.count
        desc = pltpu.make_async_remote_copy(
            src_ref=src,
            dst_ref=dst,
            send_sem=self.send_sems.at[at],
            recv_sem=self.recv_sems.at[at] if slot is None else slot,
            device_id=device,
            device_id_type=MESH,
        )
        return desc

    def start(self, src, dst, device):
        desc = self.copy(src, dst, device)
        desc.start()
        self.sent.append((None, desc))
        return desc

    def drain(self):
        for cond, desc in self.sent:
            if cond is None:
                desc.wait_send()
            else:
                pl.when(cond)(desc.wait_send)


class Gather:
    def __init__(self, links, ref, at, devs, over_y):
        self.links, self.ref, self.devs, self.over_y = links, ref, devs, over_y
        self.y, self.zh, self.x = at
        self.xs = [self.x, (self.x + 3) % 4, (self.x + 1) % 4, (self.x + 2) % 4]
        self.first = {}
        self.second = {}

    def view(self, zh, x, y=None):
        if not self.over_y:
            return self.ref.at[zh, x]
        return self.ref.at[self.y if y is None else y, zh, x]

    def pair(self, x, y):
        return self.ref.at[y, :, x]

    def send(self, view, to):
        return self.links.start(view, view, self.devs[to])

    def start(self):
        own = self.view(self.zh, self.x)
        self.z = self.send(own, "zh")
        self.a_right = self.send(own, "right")
        self.a_left = self.send(own, "left")

    def after_z(self):
        self.z.wait_recv()
        other = self.view(1 - self.zh, self.x)
        self.b_right = self.send(other, "right")
        self.b_left = self.send(other, "left")

    def forward_x(self):
        self.a_right.wait_recv()
        self.f_right = self.send(self.view(self.zh, self.xs[1]), "right")
        self.b_left.wait_recv()
        self.f_left = self.send(self.view(1 - self.zh, self.xs[2]), "left")

    def wait_x1(self):
        self.b_right.wait_recv()
        self.a_left.wait_recv()

    def wait_x2(self):
        self.f_right.wait_recv()
        self.f_left.wait_recv()

    def start_y(self, g):
        block = self.pair(self.xs[g], self.y)
        self.first[g] = (self.send(block, "up"), self.send(block, "down"))

    def forward_y(self, g):
        up, down = self.first[g]
        up.wait_recv()
        a = self.send(self.ref.at[(self.y + 3) % 4, 0, self.xs[g]], "up")
        down.wait_recv()
        b = self.send(self.ref.at[(self.y + 1) % 4, 1, self.xs[g]], "down")
        self.second[g] = (a, b)

    def wait_y(self, g):
        for desc in self.second[g]:
            desc.wait_recv()


LINKS = 96


def kernel(
    fs, ft, wd32, wc32, wu32, out_s, out_t,
    ff, taps, wd_own, wd, wc, wu, part, part_in, first, first_z, apad, acc, sums, sums_in,
    top, up_acc, spread, send_sems, recv_sems, plane_sems, sum_sems, local_sem,
):
    p = lax.axis_index("param")
    s = lax.axis_index("space")
    zl, c = p // 2, p % 2
    y, zh, x = s // 8, (s // 4) % 2, s % 4

    def space(yy, zz, xx):
        return 8 * yy + 4 * zz + xx

    sib = (2 * zl + 1 - c, s)
    across = (2 * (1 - zl) + c, s)
    swap = (2 * (1 - zl) + c, space((y + 2) % 4, zh, x))
    devs = {
        "zh": (p, space(y, 1 - zh, x)),
        "right": (p, space(y, zh, (x + 1) % 4)),
        "left": (p, space(y, zh, (x + 3) % 4)),
        "up": (p, space((y + 1) % 4, zh, x)),
        "down": (p, space((y + 3) % 4, zh, x)),
    }
    partners = [sib, across, swap] + list(devs.values())
    barrier = pltpu.get_barrier_semaphore()
    for device in partners:
        pl.semaphore_signal(barrier, inc=1, device_id=device, device_id_type=MESH)

    placed = (y // 2) == zl
    wd_own[...] = wd32[...].astype(BF16)

    @pl.when(placed)
    def _():
        wd[y, zh, x] = wd_own[...]

    pl.semaphore_wait(barrier, len(partners))
    links = Links(send_sems, recv_sems, LINKS)

    moved = links.copy(wd_own, wd.at[(y + 2) % 4, zh, x], swap)
    links.sent.append((jnp.logical_not(placed), moved))
    pl.when(jnp.logical_not(placed))(moved.start)

    for f, fine in enumerate((fs, ft)):
        ff[...] = fine[...].astype(F32)
        for dz in range(2):
            for dy in range(2):
                for dx in range(2):
                    rows = ff[dz, :, dy, pl.ds(dx, 32, stride=2), :]
                    taps[c, 4 * dz + 2 * dy + dx, f] = rows.reshape(256, 128).astype(BF16)

    pl.when(jnp.logical_not(placed))(moved.wait_recv)
    at = (y, zh, x)
    gd = Gather(links, wd, at, devs, True)
    gc = Gather(links, wc, at, devs, False)
    gu = Gather(links, wu, at, devs, True)
    gd.start()
    fine_copy = links.start(taps.at[c], taps.at[c], sib)
    wc[zh, x] = wc32[...].astype(BF16)
    for t in range(4):
        for dx in range(2):
            wu[y, zh, x, t, :, 128 * dx : 128 * dx + 128] = wu32[2 * t + dx].astype(BF16)
    gd.after_z()
    gd.start_y(0)
    gd.forward_x()
    gd.wait_x1()
    gd.start_y(1)
    gd.start_y(2)
    gd.wait_x2()
    gd.start_y(3)
    gc.start()
    gd.forward_y(0)
    gd.forward_y(1)
    gd.forward_y(2)
    gc.after_z()
    gu.start()
    gd.forward_y(3)
    gu.after_z()
    fine_copy.wait_recv()
    for g in range(4):
        gd.wait_y(g)

    def down(half):
        total = None
        for t in range(8):
            rows = jnp.concatenate([taps[0, t], taps[1, t]], axis=-1).reshape(512, 256)
            weights = wd[pl.ds(2 * half, 2), :, :, t].reshape(256, 256)
            term = jnp.dot(rows, weights, preferred_element_type=F32)
            total = term if total is None else total + term
        return total

    part[...] = down(1 - zl).astype(BF16)
    part_copy = links.start(part, part_in, across)
    gc.forward_x()
    gu.forward_x()
    acc[0] = down(zl)
    gu.start_y(0)
    gu.wait_x1()
    gu.start_y(1)
    gu.start_y(2)
    part_copy.wait_recv()
    val, dir_ = silu_pair(
        acc[0, :256] + part_in[:256].astype(F32), acc[0, 256:] + part_in[256:].astype(F32)
    )
    first[0] = val.astype(BF16).reshape(8, 32, 256)
    first[1] = dir_.astype(BF16).reshape(8, 32, 256)
    first_copy = links.start(first, first_z, across)

    apad[:, :, pl.ds(0, 1)] = jnp.zeros((2, 6, 1, 32, 256), BF16)
    apad[:, :, pl.ds(9, 1)] = jnp.zeros((2, 6, 1, 32, 256), BF16)
    last_group = jnp.logical_and(x == 3, zh == 1)
    first_group = jnp.logical_and(x == 0, zh == 0)

    @pl.when(first_group)
    def _():
        apad[:, 0, pl.ds(1, 8)] = jnp.zeros((2, 8, 32, 256), BF16)

    @pl.when(last_group)
    def _():
        apad[:, 5, pl.ds(1, 8)] = jnp.zeros((2, 8, 32, 256), BF16)

    def window(slot):
        return apad.at[:, slot, pl.ds(1, 8)]

    def spread_planes(block, chunk):
        here = jnp.logical_and(chunk == y, x == y)
        main = links.copy(block, window(x + 1), (p, space(chunk, zh, y)), plane_sems.at[x + 1])
        away = jnp.logical_not(here)
        links.sent.append((away, main))
        pl.when(away)(main.start)

        @pl.when(here)
        def _():
            same = pltpu.make_async_copy(block, window(x + 1), local_sem)
            same.start()
            same.wait()

        after = jnp.logical_and(x == 3, s != 31)
        group = (s + 1) // 4
        high = links.copy(
            block, window(0), (p, space(chunk, group % 2, (group // 2) % 4)), plane_sems.at[0]
        )
        links.sent.append((after, high))
        pl.when(after)(high.start)
        before = jnp.logical_and(x == 0, s != 0)
        group = (s + 31) // 4
        low = links.copy(
            block, window(5), (p, space(chunk, group % 2, (group // 2) % 4)), plane_sems.at[5]
        )
        links.sent.append((before, low))
        pl.when(before)(low.start)

    spread_planes(first, p)
    gu.wait_x2()
    gu.start_y(3)
    first_copy.wait_recv()
    spread_planes(first_z, 2 * (1 - zl) + c)
    gc.wait_x1()
    gc.wait_x2()

    gets = c == y % 2
    for slot in range(6):
        hop = links.copy(window(slot), window(slot), sib, plane_sems.at[slot])
        arrives = None
        if slot == 0:
            arrives = jnp.logical_not(first_group)
        elif slot == 5:
            arrives = jnp.logical_not(last_group)
        else:
            inside = jnp.logical_and(x == slot - 1, y == slot - 1)
            arrives = jnp.logical_not(jnp.logical_and(gets, inside))
        pl.when(arrives)(hop.wait_recv)
        sends = gets
        if slot == 0:
            sends = jnp.logical_and(gets, jnp.logical_not(first_group))
        if slot == 5:
            sends = jnp.logical_and(gets, jnp.logical_not(last_group))
        links.sent.append((sends, hop))
        pl.when(sends)(hop.start)

    for g in range(4):
        gu.forward_y(g)

    edge = lax.broadcasted_iota(jnp.int32, (1, 32, 1), 1)

    for plane in range(4):
        for kz in range(3):
            for ky in range(3):
                rows = apad[:, plane + kz, ky : ky + 8].reshape(512, 256)
                for kx in range(3):
                    weights = wc[:, :, 9 * kz + 3 * ky + kx].reshape(256, 256)
                    term = jnp.dot(rows, weights, preferred_element_type=F32)
                    if kz == 0 and ky == 0:
                        acc[kx] = term
                    else:
                        acc[kx] += term
        low = pltpu.roll(acc[0], 1, 0).reshape(16, 32, 256)
        high = pltpu.roll(acc[2], 511, 0).reshape(16, 32, 256)
        total = acc[1].reshape(16, 32, 256)
        total = total + jnp.where(edge == 0, 0.0, low) + jnp.where(edge == 31, 0.0, high)
        sums[plane] = total.reshape(512, 256).astype(BF16)
        mine = jnp.logical_and(y == x, x == plane)
        away = jnp.logical_not(mine)
        part_sum = links.copy(
            sums.at[plane], sums_in.at[y], (p, space(x, zh, plane)), sum_sems.at[y]
        )
        links.sent.append((away, part_sum))
        pl.when(away)(part_sum.start)

        @pl.when(mine)
        def _():
            same = pltpu.make_async_copy(sums.at[plane], sums_in.at[y], local_sem)
            same.start()
            same.wait()

    for g in range(4):
        gu.wait_y(g)
    for k in range(4):
        mine = jnp.logical_and(y == x, y == k)
        desc = pltpu.make_async_remote_copy(
            src_ref=sums.at[0], dst_ref=sums_in.at[k], send_sem=send_sems.at[0],
            recv_sem=sum_sems.at[k], device_id=sib, device_id_type=MESH,
        )
        pl.when(jnp.logical_not(mine))(desc.wait_recv)

    total = sums_in[0].astype(F32) + sums_in[1].astype(F32)
    total = total + (sums_in[2].astype(F32) + sums_in[3].astype(F32))
    val, dir_ = silu_pair(total[:256], total[256:])
    top[p, :256] = (val + first[0].reshape(256, 256).astype(F32)).astype(BF16)
    top[p, 256:] = (dir_ + first[1].reshape(256, 256).astype(F32)).astype(BF16)
    cross = links.start(top.at[p], top.at[p], across)
    near = links.start(top.at[p], top.at[p], sib)

    def add_up(chunk, fresh):
        rows = top[chunk]
        for t in range(4):
            weights = wu[chunk, :, :, t].reshape(256, 256)
            term = jnp.dot(rows, weights, preferred_element_type=F32)
            if fresh:
                up_acc[t] = term
            else:
                up_acc[t] += term

    add_up(p, True)
    near.wait_recv()
    add_up(sib[0], False)
    cross.wait_recv()
    relay = links.start(top.at[across[0]], top.at[across[0]], sib)
    add_up(across[0], False)
    relay.wait_recv()
    add_up(2 * (1 - zl) + 1 - c, False)
    for f, out in enumerate((out_s, out_t)):
        for t in range(4):
            for dx in range(2):
                block = up_acc[t, 256 * f : 256 * f + 256, 128 * dx : 128 * dx + 128]
                spread[t // 2, :, t % 2, pl.ds(dx, 32, stride=2), :] = block.reshape(8, 32, 128)
        out[...] = spread[...].astype(BF16)
    links.drain()


def local(fine_state, fine_tangent, down_weight, conv_weight, up_weight):
    vmem = pl.BlockSpec(memory_space=pltpu.VMEM)
    fine = (2, 8, 2, 64, 128)
    shape = jax.ShapeDtypeStruct(fine, BF16)
    state, tangent = pl.pallas_call(
        kernel,
        out_shape=(shape, shape),
        in_specs=[vmem] * 5,
        out_specs=(vmem, vmem),
        scratch_shapes=[
            pltpu.VMEM(fine, F32),
            pltpu.VMEM((2, 8, 2, 256, 128), BF16),
            pltpu.VMEM((8, 16, 256), BF16),
            pltpu.VMEM((4, 2, 4, 8, 16, 256), BF16),
            pltpu.VMEM((2, 4, 27, 32, 256), BF16),
            pltpu.VMEM((4, 2, 4, 4, 32, 256), BF16),
            pltpu.VMEM((512, 256), BF16),
            pltpu.VMEM((512, 256), BF16),
            pltpu.VMEM((2, 8, 32, 256), BF16),
            pltpu.VMEM((2, 8, 32, 256), BF16),
            pltpu.VMEM((2, 6, 10, 32, 256), BF16),
            pltpu.VMEM((3, 512, 256), F32),
            pltpu.VMEM((4, 512, 256), BF16),
            pltpu.VMEM((4, 512, 256), BF16),
            pltpu.VMEM((4, 512, 256), BF16),
            pltpu.VMEM((4, 512, 256), F32),
            pltpu.VMEM(fine, F32),
            pltpu.SemaphoreType.DMA((LINKS,)),
            pltpu.SemaphoreType.DMA((LINKS,)),
            pltpu.SemaphoreType.DMA((6,)),
            pltpu.SemaphoreType.DMA((4,)),
            pltpu.SemaphoreType.DMA,
        ],
        compiler_params=pltpu.CompilerParams(
            collective_id=0, has_side_effects=True, vmem_limit_bytes=56 * 2**20
        ),
    )(fine_state.reshape(fine), fine_tangent.reshape(fine), down_weight, conv_weight, up_weight)
    return state.reshape(fine_state.shape), tangent.reshape(fine_state.shape)


def solution(mesh):
    in_specs = (
        P("space", None, None, "param"),
        P("space", None, None, "param"),
        P(None, "space", "param"),
        P(None, "space", "param"),
        P(None, "space", "param"),
    )
    out_specs = (P("space", None, None, "param"), P("space", None, None, "param"))
    return jax.shard_map(local, mesh=mesh, in_specs=in_specs, out_specs=out_specs, check_vma=False)
```

time: 473 us -> 136 us (0.29)
  the two profiles are of different devices: /device:TPU:5 before, /device:TPU:47 now
where the time goes in v1:
time: 136 us
  Pallas kernels  133 us (98%)
  local copies, waits for them, and re-layouts  2.72 us (2%)
    pallas_call x1, Pallas kernels, local(): pl.pallas_call(kernel, out_shape=(shape, shape), in_specs=[vmem] * 5, out...  133 us
    unnamed x4, local copies, waits for them, and re-layouts  2.72 us

profile of v1, /device:TPU:47, one launch (start us, length us, event | category | flops | bytes accessed | tf_op | source)
XLA Modules:
  0.0 135.9 jit_solution(10750769761772252713)
XLA Ops:
  0.6 132.6 %shard_map.68 = (bf16[2,8,2,64,128]{4,3,2,1,0:T(8,128)(2,1)}, bf16[2,8,2,64,128]{4,3,2,1,0:T(8,128)(2,1)}) custom-call(bf16[2,8,2,64,128]{4,3,2,1,0:T(8,128)(2,1)} %bitcast.6, bf16[2,8,2,64,128]{4,3,2,1,0:T(8,128)(2,1)} %bitcast.7, f32[8,16,256]{2,1,0:T(8,128)} %wd32.1, f32[27,32,256]{2,1,0:T(8,128)} %wc32.1, f32[8,32,128]{2,1,0:T(8,128)} %wu32.1), custom_call_target="tpu_custom_call" | custom-call | tf_op jit(solution)/shard_map/pallas_call | solution.py:380
  133.2 0.0 copy-start
  133.2 1.9 %copy.9 = bf16[2,16,64,128]{3,2,1,0:T(8,128)(2,1)} copy(bf16[2,16,64,128]{3,2,1,0:T(8,128)(2,1)} %bitcast.5) | data formatting | bytes 1048576
  135.1 0.0 copy-done
  135.1 0.8 copy.10
Async XLA Ops:
  133.2 1.9 %copy-start = (bf16[2,8,2,64,128]{4,3,2,1,0:T(8,128)(2,1)S(1)}, bf16[2,8,2,64,128]{4,3,2,1,0:T(8,128)(2,1)}, u32[]{:S(2)}) copy-start(bf16[2,8,2,64,128]{4,3,2,1,0:T(8,128)(2,1)} %get-tuple-element.5) | copy-start | bytes 1572868

commit v2 on v1

v2 whole, which is shorter than its diff:
```python
import jax
import jax.numpy as jnp
from jax import lax
from jax.experimental import pallas as pl
from jax.experimental.pallas import tpu as pltpu
from jax.sharding import PartitionSpec as P

MESH = pl.DeviceIdType.MESH
F32 = jnp.float32
BF16 = jnp.bfloat16


def silu_pair(primal, tangent):
    sigma = jax.nn.sigmoid(primal)
    return primal * sigma, sigma * (1.0 + primal * (1.0 - sigma)) * tangent


class Links:
    def __init__(self, send_sems, recv_sems, count):
        self.send_sems, self.recv_sems, self.count = send_sems, recv_sems, count
        self.used = 0
        self.sent = []

    def copy(self, src, dst, device, slot=None):
        at = self.used
        self.used += 1
        assert self.used <= self.count
        desc = pltpu.make_async_remote_copy(
            src_ref=src,
            dst_ref=dst,
            send_sem=self.send_sems.at[at],
            recv_sem=self.recv_sems.at[at] if slot is None else slot,
            device_id=device,
            device_id_type=MESH,
        )
        return desc

    def start(self, src, dst, device):
        desc = self.copy(src, dst, device)
        desc.start()
        self.sent.append((None, desc))
        return desc

    def drain(self):
        for cond, desc in self.sent:
            if cond is None:
                desc.wait_send()
            else:
                pl.when(cond)(desc.wait_send)


class Ring:
    def __init__(self, links, view, at, to_z, up, down):
        self.links, self.view, self.to_z, self.up, self.down = links, view, to_z, up, down
        self.zh, self.a = at

    def send(self, z, a, to):
        view = self.view(z, a)
        return self.links.start(view, view, to)

    def start_z(self):
        self.z = self.send(self.zh, self.a, self.to_z)

    def start(self):
        self.own = self.send(self.zh, self.a, self.up), self.send(self.zh, self.a, self.down)

    def after_z(self):
        self.z.wait_recv()
        z = 1 - self.zh
        self.other = self.send(z, self.a, self.up), self.send(z, self.a, self.down)

    def forward(self):
        self.own[0].wait_recv()
        first = self.send(self.zh, (self.a + 3) % 4, self.up)
        self.other[1].wait_recv()
        self.far = first, self.send(1 - self.zh, (self.a + 1) % 4, self.down)

    def wait(self):
        for desc in (self.own[1], self.other[0]) + self.far:
            desc.wait_recv()


class Gather:
    def __init__(self, links, view, at, device, up, down):
        self.links, self.view, self.device, self.up, self.down = links, view, device, up, down
        self.zh, self.a, self.b = at
        self.near, self.first, self.second = {}, {}, {}

    def send(self, z, a, b, to):
        view = self.view(z, a, b)
        return self.links.start(view, view, to)

    def start(self):
        for da in (1, 3, 0, 2):
            for dz in range(2):
                if da or dz:
                    to = self.device((self.zh + dz) % 2, (self.a + da) % 4)
                    self.near[dz, da] = self.send(self.zh, self.a, self.b, to)

    def group(self, g):
        return (self.a + 4 - g) % 4

    def start_b(self, g):
        for dz in range(2):
            if g or dz:
                self.near[dz, g].wait_recv()
        a = self.group(g)
        self.first[g] = self.send(None, a, self.b, self.up), self.send(None, a, self.b, self.down)

    def forward_b(self, g):
        a = self.group(g)
        up, down = self.first[g]
        up.wait_recv()
        far = self.send(0, a, (self.b + 3) % 4, self.up)
        down.wait_recv()
        self.second[g] = far, self.send(1, a, (self.b + 1) % 4, self.down)

    def wait_b(self, g):
        for desc in self.second[g]:
            desc.wait_recv()


LINKS = 160
ORDER = (0, 1, 3, 2)


def kernel(
    fs, ft, wd32, wc32, wu32, out_s, out_t,
    ff, taps, wd_own, wd, wc, wu, part, part_in, first, first_z, mid, apad, acc, sums, sums_in,
    top, up_acc, spread, send_sems, recv_sems, mid_sems, plane_sems, sum_sems, local_sem,
):
    p = lax.axis_index("param")
    s = lax.axis_index("space")
    zl, c = p // 2, p % 2
    y, zh, x = s // 8, (s // 4) % 2, s % 4

    def space(yy, zz, xx):
        return 8 * yy + 4 * zz + xx

    sib = (2 * zl + 1 - c, s)
    across = (2 * (1 - zl) + c, s)
    swap = (2 * (1 - zl) + c, space((y + 2) % 4, zh, x))
    devs = {
        "zh": (p, space(y, 1 - zh, x)),
        "right": (p, space(y, zh, (x + 1) % 4)),
        "left": (p, space(y, zh, (x + 3) % 4)),
        "up": (p, space((y + 1) % 4, zh, x)),
        "down": (p, space((y + 3) % 4, zh, x)),
    }
    partners = [sib, across, swap]
    for dz in range(2):
        for da in range(4):
            if da or dz:
                partners.append((p, space(y, (zh + dz) % 2, (x + da) % 4)))
            if da:
                partners.append((p, space((y + da) % 4, (zh + dz) % 2, x)))
    barrier = pltpu.get_barrier_semaphore()
    for device in partners:
        pl.semaphore_signal(barrier, inc=1, device_id=device, device_id_type=MESH)

    placed = (y // 2) == zl
    wd_own[...] = wd32[...].astype(BF16)

    @pl.when(placed)
    def _():
        wd[y, zh, x] = wd_own[...]

    pl.semaphore_wait(barrier, len(partners))
    links = Links(send_sems, recv_sems, LINKS)

    moved = links.copy(wd_own, wd.at[(y + 2) % 4, zh, x], swap)
    links.sent.append((jnp.logical_not(placed), moved))
    pl.when(jnp.logical_not(placed))(moved.start)
    wc[zh, x] = wc32[...].astype(BF16)

    def pick(z):
        return slice(None) if z is None else z

    gd = (
        Gather(
            links, lambda z, a, b: wd.at[b, pick(z), a, 0:4], (zh, x, y),
            lambda z, a: (p, space(y, z, a)), devs["up"], devs["down"],
        ),
        Gather(
            links, lambda z, a, b: wd.at[a, pick(z), b, 4:8], (zh, y, x),
            lambda z, a: (p, space(a, z, x)), devs["right"], devs["left"],
        ),
    )
    gc = Ring(links, lambda z, a: wc.at[z, a], (zh, x), devs["zh"], devs["right"], devs["left"])
    gu = Gather(
        links, lambda z, a, b: wu.at[b, pick(z), a], (zh, x, y),
        lambda z, a: (p, space(y, z, a)), devs["up"], devs["down"],
    )
    pl.when(jnp.logical_not(placed))(moved.wait_recv)
    gd[0].start()
    gd[1].start()
    gc.start_z()

    def extract(f, fine):
        ff[...] = fine[...].astype(F32)
        for dz in range(2):
            for dy in range(2):
                for dx in range(2):
                    rows = ff[dz, :, dy, pl.ds(dx, 32, stride=2), :]
                    taps[c, 4 * dz + 2 * dy + dx, f] = rows.reshape(256, 128).astype(BF16)

    extract(0, fs)
    for g in ORDER:
        gd[0].start_b(g)
        gd[1].start_b(g)
    extract(1, ft)
    fine_copy = links.start(taps.at[c], taps.at[c], sib)
    for g in ORDER:
        gd[0].forward_b(g)
        gd[1].forward_b(g)
    gc.start()
    for t in range(4):
        for dx in range(2):
            wu[y, zh, x, t, :, 128 * dx : 128 * dx + 128] = wu32[2 * t + dx].astype(BF16)
    gu.start()
    gc.after_z()
    fine_copy.wait_recv()
    for g in ORDER:
        gd[0].wait_b(g)
        gd[1].wait_b(g)

    def down(half, h):
        total = None
        for t in range(8):
            rows = [taps[k, t, :, 128 * h : 128 * h + 128] for k in range(2)]
            rows = jnp.concatenate(rows, axis=-1).reshape(256, 256)
            weights = wd[pl.ds(2 * half, 2), :, :, t].reshape(256, 256)
            term = jnp.dot(rows, weights, preferred_element_type=F32)
            total = term if total is None else total + term
        return total

    part_copy = []
    for h in range(2):
        part[h] = down(1 - zl, h).astype(BF16)
        part_copy.append(links.start(part.at[h], part_in.at[h], across))
    for h in range(2):
        acc[h, :256] = down(zl, h)
    gc.forward()
    apad[:, :, pl.ds(0, 1)] = jnp.zeros((2, 6, 1, 32, 256), BF16)
    apad[:, :, pl.ds(9, 1)] = jnp.zeros((2, 6, 1, 32, 256), BF16)
    last_group = jnp.logical_and(x == 3, zh == 1)
    first_group = jnp.logical_and(x == 0, zh == 0)

    @pl.when(first_group)
    def _():
        apad[:, 0, pl.ds(1, 8)] = jnp.zeros((2, 8, 32, 256), BF16)

    @pl.when(last_group)
    def _():
        apad[:, 5, pl.ds(1, 8)] = jnp.zeros((2, 8, 32, 256), BF16)

    mids = {}

    def to_row(block, chunk, h):
        rows = pl.ds(4 * h, 4)
        move = links.copy(
            block.at[:, rows], mid.at[y, :, rows], (p, space(chunk, zh, x)), mid_sems.at[y, h]
        )
        away = chunk != y
        links.sent.append((away, move))
        pl.when(away)(move.start)

        @pl.when(chunk == y)
        def _():
            mid[y, :, rows] = block[:, rows]

    first_copy = []
    for h in range(2):
        part_copy[h].wait_recv()
        val, dir_ = silu_pair(
            acc[h, :128] + part_in[h, :128].astype(F32),
            acc[h, 128:256] + part_in[h, 128:].astype(F32),
        )
        rows = pl.ds(4 * h, 4)
        first[0, rows] = val.astype(BF16).reshape(4, 32, 256)
        first[1, rows] = dir_.astype(BF16).reshape(4, 32, 256)
        first_copy.append(links.start(first.at[:, rows], first_z.at[:, rows], across))
        to_row(first, p, h)
    for h in range(2):
        first_copy[h].wait_recv()
        to_row(first_z, 2 * (1 - zl) + c, h)

    gets = c == y % 2

    def window(slot, h):
        return apad.at[:, slot, pl.ds(1 + 4 * h, 4)]

    for h in range(2):
        for step in ORDER:
            source = (y + step) % 4
            block = mid.at[source, :, pl.ds(4 * h, 4)]
            if step:
                arrived = pltpu.make_async_remote_copy(
                    src_ref=block, dst_ref=block, send_sem=send_sems.at[0],
                    recv_sem=mid_sems.at[source, h], device_id=sib, device_id_type=MESH,
                )
                pl.when(gets)(arrived.wait_recv)
            stays = jnp.logical_and(gets, x == source)
            leaves = jnp.logical_and(gets, x != source)
            main = links.copy(
                block, window(x + 1, h), (p, space(y, zh, source)), plane_sems.at[x + 1, h]
            )
            links.sent.append((leaves, main))
            pl.when(leaves)(main.start)

            @pl.when(stays)
            def _():
                apad[:, x + 1, pl.ds(1 + 4 * h, 4)] = mid[source, :, pl.ds(4 * h, 4)]

            plane = space(source, zh, x)
            for slot, edge_x, group, end in (
                (0, 3, (plane + 1) // 4, 31), (5, 0, (plane + 31) // 4, 0)
            ):
                sends = jnp.logical_and(gets, jnp.logical_and(x == edge_x, plane != end))
                to = (p, space(y, group % 2, (group // 2) % 4))
                halo = links.copy(block, window(slot, h), to, plane_sems.at[slot, h])
                links.sent.append((sends, halo))
                pl.when(sends)(halo.start)
    gc.wait()

    for h in range(2):
        for slot in (1, 2, 3, 4, 0, 5):
            view = window(slot, h)
            hop = links.copy(view, view, sib, plane_sems.at[slot, h])
            sends = gets
            if slot == 0:
                arrives = jnp.logical_not(first_group)
                sends = jnp.logical_and(gets, arrives)
            elif slot == 5:
                arrives = jnp.logical_not(last_group)
                sends = jnp.logical_and(gets, arrives)
            else:
                arrives = jnp.logical_not(jnp.logical_and(gets, x == slot - 1))
            pl.when(arrives)(hop.wait_recv)
            links.sent.append((sends, hop))
            pl.when(sends)(hop.start)

    for g in ORDER:
        gu.start_b(g)

    edge = lax.broadcasted_iota(jnp.int32, (1, 32, 1), 1)
    for plane in range(4):
        for kx in range(3):
            total = None
            for kz in range(3):
                for ky in range(3):
                    rows = apad[:, plane + kz, ky : ky + 8].reshape(512, 256)
                    weights = wc[:, :, 9 * kz + 3 * ky + kx].reshape(256, 256)
                    term = jnp.dot(rows, weights, preferred_element_type=F32)
                    total = term if total is None else total + term
            acc[kx] = total
        low = pltpu.roll(acc[0], 1, 0).reshape(16, 32, 256)
        high = pltpu.roll(acc[2], 511, 0).reshape(16, 32, 256)
        total = acc[1].reshape(16, 32, 256)
        total = total + jnp.where(edge == 0, 0.0, low) + jnp.where(edge == 31, 0.0, high)
        sums[plane] = total.reshape(512, 256).astype(BF16)
        mine = jnp.logical_and(y == x, x == plane)
        away = jnp.logical_not(mine)
        part_sum = links.copy(
            sums.at[plane], sums_in.at[y], (p, space(x, zh, plane)), sum_sems.at[y]
        )
        links.sent.append((away, part_sum))
        pl.when(away)(part_sum.start)

        @pl.when(mine)
        def _():
            same = pltpu.make_async_copy(sums.at[plane], sums_in.at[y], local_sem)
            same.start()
            same.wait()

        gu.forward_b(ORDER[plane])

    for g in ORDER:
        gu.wait_b(g)
    for k in range(4):
        mine = jnp.logical_and(y == x, y == k)
        desc = pltpu.make_async_remote_copy(
            src_ref=sums.at[0], dst_ref=sums_in.at[k], send_sem=send_sems.at[0],
            recv_sem=sum_sems.at[k], device_id=sib, device_id_type=MESH,
        )
        pl.when(jnp.logical_not(mine))(desc.wait_recv)

    total = sums_in[0].astype(F32) + sums_in[1].astype(F32)
    total = total + (sums_in[2].astype(F32) + sums_in[3].astype(F32))
    val, dir_ = silu_pair(total[:256], total[256:])
    top[p, :256] = (val + first[0].reshape(256, 256).astype(F32)).astype(BF16)
    top[p, 256:] = (dir_ + first[1].reshape(256, 256).astype(F32)).astype(BF16)
    cross = links.start(top.at[p], top.at[p], across)
    near = links.start(top.at[p], top.at[p], sib)

    def add_up(chunk, fresh):
        rows = top[chunk]
        for t in range(4):
            weights = wu[chunk, :, :, t].reshape(256, 256)
            term = jnp.dot(rows, weights, preferred_element_type=F32)
            if fresh:
                up_acc[t] = term
            else:
                up_acc[t] += term

    add_up(p, True)
    near.wait_recv()
    add_up(sib[0], False)
    cross.wait_recv()
    relay = links.start(top.at[across[0]], top.at[across[0]], sib)
    add_up(across[0], False)
    relay.wait_recv()
    add_up(2 * (1 - zl) + 1 - c, False)
    for f, out in enumerate((out_s, out_t)):
        for t in range(4):
            for dx in range(2):
                block = up_acc[t, 256 * f : 256 * f + 256, 128 * dx : 128 * dx + 128]
                spread[t // 2, :, t % 2, pl.ds(dx, 32, stride=2), :] = block.reshape(8, 32, 128)
        out[...] = spread[...].astype(BF16)
    links.drain()


def local(fine_state, fine_tangent, down_weight, conv_weight, up_weight):
    vmem = pl.BlockSpec(memory_space=pltpu.VMEM)
    fine = (2, 8, 2, 64, 128)
    shape = jax.ShapeDtypeStruct(fine, BF16)
    state, tangent = pl.pallas_call(
        kernel,
        out_shape=(shape, shape),
        in_specs=[vmem] * 5,
        out_specs=(vmem, vmem),
        scratch_shapes=[
            pltpu.VMEM(fine, F32),
            pltpu.VMEM((2, 8, 2, 256, 128), BF16),
            pltpu.VMEM((8, 16, 256), BF16),
            pltpu.VMEM((4, 2, 4, 8, 16, 256), BF16),
            pltpu.VMEM((2, 4, 27, 32, 256), BF16),
            pltpu.VMEM((4, 2, 4, 4, 32, 256), BF16),
            pltpu.VMEM((2, 256, 256), BF16),
            pltpu.VMEM((2, 256, 256), BF16),
            pltpu.VMEM((2, 8, 32, 256), BF16),
            pltpu.VMEM((2, 8, 32, 256), BF16),
            pltpu.VMEM((4, 2, 8, 32, 256), BF16),
            pltpu.VMEM((2, 6, 10, 32, 256), BF16),
            pltpu.VMEM((3, 512, 256), F32),
            pltpu.VMEM((4, 512, 256), BF16),
            pltpu.VMEM((4, 512, 256), BF16),
            pltpu.VMEM((4, 512, 256), BF16),
            pltpu.VMEM((4, 512, 256), F32),
            pltpu.VMEM(fine, F32),
            pltpu.SemaphoreType.DMA((LINKS,)),
            pltpu.SemaphoreType.DMA((LINKS,)),
            pltpu.SemaphoreType.DMA((4, 2)),
            pltpu.SemaphoreType.DMA((6, 2)),
            pltpu.SemaphoreType.DMA((4,)),
            pltpu.SemaphoreType.DMA,
        ],
        compiler_params=pltpu.CompilerParams(
            collective_id=0, has_side_effects=True, vmem_limit_bytes=56 * 2**20
        ),
    )(fine_state.reshape(fine), fine_tangent.reshape(fine), down_weight, conv_weight, up_weight)
    return state.reshape(fine_state.shape), tangent.reshape(fine_state.shape)


def solution(mesh):
    in_specs = (
        P("space", None, None, "param"),
        P("space", None, None, "param"),
        P(None, "space", "param"),
        P(None, "space", "param"),
        P(None, "space", "param"),
    )
    out_specs = (P("space", None, None, "param"), P("space", None, None, "param"))
    return jax.shard_map(local, mesh=mesh, in_specs=in_specs, out_specs=out_specs, check_vma=False)
```

time: 136 us -> 131 us (0.963)
  Pallas kernels: 133 us -> 127 us
    pallas_call x1, Pallas kernels: 133 us -> 127 us  [local(): pl.pallas_call(kernel, out_shape=(shape, shape), in_specs=[vmem] * 5, out...]
where the time goes in v2:
time: 131 us
  Pallas kernels  127 us (97%)
  local copies, waits for them, and re-layouts  2.72 us (2%)
    pallas_call x1, Pallas kernels, local(): pl.pallas_call(kernel, out_shape=(shape, shape), in_specs=[vmem] * 5, out...  127 us
    unnamed x4, local copies, waits for them, and re-layouts  2.72 us

profile of v2, /device:TPU:47, one launch (start us, length us, event | category | flops | bytes accessed | tf_op | source)
XLA Modules:
  0.0 130.7 jit_solution(18068022612525324518)
XLA Ops:
  0.6 127.3 %shard_map.68 = (bf16[2,8,2,64,128]{4,3,2,1,0:T(8,128)(2,1)}, bf16[2,8,2,64,128]{4,3,2,1,0:T(8,128)(2,1)}) custom-call(bf16[2,8,2,64,128]{4,3,2,1,0:T(8,128)(2,1)} %bitcast.6, bf16[2,8,2,64,128]{4,3,2,1,0:T(8,128)(2,1)} %bitcast.7, f32[8,16,256]{2,1,0:T(8,128)} %wd32.1, f32[27,32,256]{2,1,0:T(8,128)} %wc32.1, f32[8,32,128]{2,1,0:T(8,128)} %wu32.1), custom_call_target="tpu_custom_call" | custom-call | tf_op jit(solution)/shard_map/pallas_call | solution.py:427
  127.9 0.0 copy-start
  127.9 1.9 %copy.9 = bf16[2,16,64,128]{3,2,1,0:T(8,128)(2,1)} copy(bf16[2,16,64,128]{3,2,1,0:T(8,128)(2,1)} %bitcast.5) | data formatting | bytes 1048576
  129.9 0.0 copy-done
  129.9 0.8 copy.10
Async XLA Ops:
  127.9 1.9 %copy-start = (bf16[2,8,2,64,128]{4,3,2,1,0:T(8,128)(2,1)S(1)}, bf16[2,8,2,64,128]{4,3,2,1,0:T(8,128)(2,1)}, u32[]{:S(2)}) copy-start(bf16[2,8,2,64,128]{4,3,2,1,0:T(8,128)(2,1)} %get-tuple-element.5) | copy-start | bytes 1572868

commit v3 on v2

v3 whole, which is shorter than its diff:
```python
import jax
import jax.numpy as jnp
from jax import lax
from jax.experimental import pallas as pl
from jax.experimental.pallas import tpu as pltpu
from jax.sharding import PartitionSpec as P

MESH = pl.DeviceIdType.MESH
F32 = jnp.float32
BF16 = jnp.bfloat16


def silu_gain(primal):
    sigma = jax.nn.sigmoid(primal)
    return primal * sigma, sigma * (1.0 + primal * (1.0 - sigma))


class Links:
    def __init__(self, send_sems, recv_sems, count):
        self.send_sems, self.recv_sems, self.count = send_sems, recv_sems, count
        self.used = 0
        self.sent = []

    def copy(self, src, dst, device, slot=None):
        at = self.used
        self.used += 1
        assert self.used <= self.count
        desc = pltpu.make_async_remote_copy(
            src_ref=src,
            dst_ref=dst,
            send_sem=self.send_sems.at[at],
            recv_sem=self.recv_sems.at[at] if slot is None else slot,
            device_id=device,
            device_id_type=MESH,
        )
        return desc

    def start(self, src, dst, device):
        desc = self.copy(src, dst, device)
        desc.start()
        self.sent.append((None, desc))
        return desc

    def drain(self):
        for cond, desc in self.sent:
            if cond is None:
                desc.wait_send()
            else:
                pl.when(cond)(desc.wait_send)


class Ring:
    def __init__(self, links, view, at, to_z, up, down):
        self.links, self.view, self.to_z, self.up, self.down = links, view, to_z, up, down
        self.zh, self.a = at

    def send(self, z, a, to):
        view = self.view(z, a)
        return self.links.start(view, view, to)

    def start_z(self):
        self.z = self.send(self.zh, self.a, self.to_z)

    def start(self):
        self.own = self.send(self.zh, self.a, self.up), self.send(self.zh, self.a, self.down)

    def after_z(self):
        self.z.wait_recv()
        z = 1 - self.zh
        self.other = self.send(z, self.a, self.up), self.send(z, self.a, self.down)

    def forward(self):
        self.own[0].wait_recv()
        first = self.send(self.zh, (self.a + 3) % 4, self.up)
        self.other[1].wait_recv()
        self.far = first, self.send(1 - self.zh, (self.a + 1) % 4, self.down)

    def wait(self):
        for desc in (self.own[1], self.other[0]) + self.far:
            desc.wait_recv()


class Gather:
    def __init__(self, links, view, at, to_z, to_a, up, down):
        self.links, self.view, self.up, self.down = links, view, up, down
        self.to_z, self.to_a = to_z, to_a
        self.zh, self.a, self.b = at
        self.near, self.first, self.second = {}, {}, {}

    def send(self, z, a, b, to):
        view = self.view(z, a, b)
        return self.links.start(view, view, to)

    def start(self):
        self.near[1, 0] = self.send(self.zh, self.a, self.b, self.to_z)
        for da in (1, 3, 2):
            self.near[0, da] = self.send(self.zh, self.a, self.b, self.to_a((self.a + da) % 4))

    def after_z(self):
        self.near[1, 0].wait_recv()
        for da in (1, 3, 2):
            self.near[1, da] = self.send(1 - self.zh, self.a, self.b, self.to_a((self.a + da) % 4))

    def group(self, g):
        return (self.a + 4 - g) % 4

    def start_b(self, g):
        if g:
            self.near[0, g].wait_recv()
            self.near[1, g].wait_recv()
        a = self.group(g)
        self.first[g] = self.send(None, a, self.b, self.up), self.send(None, a, self.b, self.down)

    def forward_b(self, g):
        a = self.group(g)
        up, down = self.first[g]
        up.wait_recv()
        far = self.send(0, a, (self.b + 3) % 4, self.up)
        down.wait_recv()
        self.second[g] = far, self.send(1, a, (self.b + 1) % 4, self.down)

    def wait_b(self, g):
        for desc in self.second[g]:
            desc.wait_recv()


LINKS = 160
SPLIT = 6
ORDER = (0, 1, 3, 2)


def kernel(
    fs, ft, wd32, wc32, wu32, out_s, out_t,
    ff, taps, wd_own, wd, wc, wu, part, part_in, first, first_z, mid, apad, acc, keep, sums, sums_in,
    top, up_acc, spread, send_sems, recv_sems, mid_sems, plane_sems, sum_sems,
):
    p = lax.axis_index("param")
    s = lax.axis_index("space")
    zl, c = p // 2, p % 2
    y, zh, x = s // 8, (s // 4) % 2, s % 4

    def space(yy, zz, xx):
        return 8 * yy + 4 * zz + xx

    sib = (2 * zl + 1 - c, s)
    across = (2 * (1 - zl) + c, s)
    swap = (2 * (1 - zl) + c, space((y + 2) % 4, zh, x))
    devs = {
        "zh": (p, space(y, 1 - zh, x)),
        "right": (p, space(y, zh, (x + 1) % 4)),
        "left": (p, space(y, zh, (x + 3) % 4)),
        "up": (p, space((y + 1) % 4, zh, x)),
        "down": (p, space((y + 3) % 4, zh, x)),
    }
    partners = [sib, across, swap]
    partners.append(devs["zh"])
    for step in range(1, 4):
        partners.append((p, space(y, zh, (x + step) % 4)))
        partners.append((p, space((y + step) % 4, zh, x)))
    barrier = pltpu.get_barrier_semaphore()
    for device in partners:
        pl.semaphore_signal(barrier, inc=1, device_id=device, device_id_type=MESH)

    placed = (y // 2) == zl
    wd_own[...] = wd32[...].astype(BF16)

    @pl.when(placed)
    def _():
        wd[y, zh, x] = wd_own[...]

    pl.semaphore_wait(barrier, len(partners))
    links = Links(send_sems, recv_sems, LINKS)

    moved = links.copy(wd_own, wd.at[(y + 2) % 4, zh, x], swap)
    links.sent.append((jnp.logical_not(placed), moved))
    pl.when(jnp.logical_not(placed))(moved.start)
    wc[zh, x] = wc32[...].astype(BF16)

    def pick(z):
        return slice(None) if z is None else z

    gd = (
        Gather(
            links, lambda z, a, b: wd.at[b, pick(z), a, :SPLIT], (zh, x, y),
            devs["zh"], lambda a: (p, space(y, zh, a)), devs["up"], devs["down"],
        ),
        Gather(
            links, lambda z, a, b: wd.at[a, pick(z), b, SPLIT:], (zh, y, x),
            devs["zh"], lambda a: (p, space(a, zh, x)), devs["right"], devs["left"],
        ),
    )
    gc = Ring(links, lambda z, a: wc.at[z, a], (zh, x), devs["zh"], devs["right"], devs["left"])
    gu = Gather(
        links, lambda z, a, b: wu.at[b, pick(z), a], (zh, x, y),
        devs["zh"], lambda a: (p, space(y, zh, a)), devs["up"], devs["down"],
    )
    gc.start_z()
    gc.start()

    for f, fine in enumerate((fs, ft)):
        ff[...] = fine[...].astype(F32)
        for dz in range(2):
            for dy in range(2):
                for dx in range(2):
                    rows = ff[dz, :, dy, pl.ds(dx, 32, stride=2), :]
                    taps[c, 4 * dz + 2 * dy + dx, f] = rows.reshape(256, 128).astype(BF16)
    fine_copy = links.start(taps.at[c], taps.at[c], sib)
    pl.when(jnp.logical_not(placed))(moved.wait_recv)
    for part_of in gd:
        part_of.start()
    for t in range(4):
        for dx in range(2):
            wu[y, zh, x, t, :, 128 * dx : 128 * dx + 128] = wu32[2 * t + dx].astype(BF16)
    for part_of in gd:
        part_of.after_z()
    for g in ORDER:
        gd[0].start_b(g)
        gd[1].start_b(g)
    gc.after_z()
    for g in ORDER:
        gd[0].forward_b(g)
        gd[1].forward_b(g)
    gu.start()
    gc.forward()
    fine_copy.wait_recv()
    for g in ORDER:
        gd[0].wait_b(g)
        gd[1].wait_b(g)

    def down(half, f):
        total = None
        for t in range(8):
            rows = jnp.concatenate([taps[0, t, f], taps[1, t, f]], axis=-1)
            weights = wd[pl.ds(2 * half, 2), :, :, t].reshape(256, 256)
            term = jnp.dot(rows, weights, preferred_element_type=F32)
            total = term if total is None else total + term
        return total

    part_copy = []
    for f in range(2):
        part[f] = down(1 - zl, f).astype(BF16)
        part_copy.append(links.start(part.at[f], part_in.at[f], across))
    for f in range(2):
        acc[f, :256] = down(zl, f)
    gu.after_z()
    apad[:, :, pl.ds(0, 1)] = jnp.zeros((2, 6, 1, 32, 256), BF16)
    apad[:, :, pl.ds(9, 1)] = jnp.zeros((2, 6, 1, 32, 256), BF16)
    last_group = jnp.logical_and(x == 3, zh == 1)
    first_group = jnp.logical_and(x == 0, zh == 0)

    @pl.when(first_group)
    def _():
        apad[:, 0, pl.ds(1, 8)] = jnp.zeros((2, 8, 32, 256), BF16)

    @pl.when(last_group)
    def _():
        apad[:, 5, pl.ds(1, 8)] = jnp.zeros((2, 8, 32, 256), BF16)

    def to_row(block, chunk, f):
        move = links.copy(
            block.at[f], mid.at[y, f], (p, space(chunk, zh, x)), mid_sems.at[y, f]
        )
        away = chunk != y
        links.sent.append((away, move))
        pl.when(away)(move.start)

        @pl.when(chunk == y)
        def _():
            mid[y, f] = block[f]

    first_copy = []
    for f in range(2):
        part_copy[f].wait_recv()
        pre = acc[f, :256] + part_in[f].astype(F32)
        if f == 0:
            value, gain = silu_gain(pre)
            acc[2, :256] = gain
        else:
            value = acc[2, :256] * pre
        first[f] = value.astype(BF16).reshape(8, 32, 256)
        first_copy.append(links.start(first.at[f], first_z.at[f], across))
        to_row(first, p, f)
    for f in range(2):
        first_copy[f].wait_recv()
        to_row(first_z, 2 * (1 - zl) + c, f)
    for g in ORDER:
        gu.start_b(g)

    gets = c == y % 2

    def window(slot, f):
        return apad.at[f, slot, pl.ds(1, 8)]

    def to_column(f):
        for step in ORDER:
            source = (y + step) % 4
            block = mid.at[source, f]
            if step:
                arrived = pltpu.make_async_remote_copy(
                    src_ref=block, dst_ref=block, send_sem=send_sems.at[0],
                    recv_sem=mid_sems.at[source, f], device_id=sib, device_id_type=MESH,
                )
                pl.when(gets)(arrived.wait_recv)
            stays = jnp.logical_and(gets, x == source)
            leaves = jnp.logical_and(gets, x != source)
            main = links.copy(
                block, window(x + 1, f), (p, space(y, zh, source)), plane_sems.at[x + 1, f]
            )
            links.sent.append((leaves, main))
            pl.when(leaves)(main.start)

            @pl.when(stays)
            def _():
                apad[f, x + 1, pl.ds(1, 8)] = mid[source, f]

            plane = space(source, zh, x)
            for slot, edge_x, group, end in (
                (0, 3, (plane + 1) // 4, 31), (5, 0, (plane + 31) // 4, 0)
            ):
                sends = jnp.logical_and(gets, jnp.logical_and(x == edge_x, plane != end))
                to = (p, space(y, group % 2, (group // 2) % 4))
                halo = links.copy(block, window(slot, f), to, plane_sems.at[slot, f])
                links.sent.append((sends, halo))
                pl.when(sends)(halo.start)

    def to_sibling(f):
        for slot in (1, 2, 3, 4, 0, 5):
            view = window(slot, f)
            hop = links.copy(view, view, sib, plane_sems.at[slot, f])
            sends = gets
            if slot == 0:
                arrives = jnp.logical_not(first_group)
                sends = jnp.logical_and(gets, arrives)
            elif slot == 5:
                arrives = jnp.logical_not(last_group)
                sends = jnp.logical_and(gets, arrives)
            else:
                arrives = jnp.logical_not(jnp.logical_and(gets, x == slot - 1))
            pl.when(arrives)(hop.wait_recv)
            links.sent.append((sends, hop))
            pl.when(sends)(hop.start)

    edge = lax.broadcasted_iota(jnp.int32, (1, 32, 1), 1)

    def convolve(f, pair):
        for kx in range(3):
            total = None
            for kz in range(3):
                for ky in range(3):
                    rows = apad[f, pl.ds(2 * pair + kz, 2), ky : ky + 8].reshape(512, 256)
                    weights = wc[:, :, 9 * kz + 3 * ky + kx].reshape(256, 256)
                    term = jnp.dot(rows, weights, preferred_element_type=F32)
                    total = term if total is None else total + term
            acc[kx] = total
        low = pltpu.roll(acc[0], 1, 0).reshape(16, 32, 256)
        high = pltpu.roll(acc[2], 511, 0).reshape(16, 32, 256)
        total = acc[1].reshape(16, 32, 256)
        total = total + jnp.where(edge == 0, 0.0, low) + jnp.where(edge == 31, 0.0, high)
        sums[f, pl.ds(2 * pair, 2)] = total.reshape(2, 256, 256).astype(BF16)
        for plane in (2 * pair, 2 * pair + 1):
            mine = jnp.logical_and(y == x, x == plane)
            away = jnp.logical_not(mine)
            move = links.copy(
                sums.at[f, plane], sums_in.at[f, y], (p, space(x, zh, plane)), sum_sems.at[f, y]
            )
            links.sent.append((away, move))
            pl.when(away)(move.start)

            @pl.when(mine)
            def _():
                sums_in[f, y] = sums[f, plane]

    def gather_sums(f):
        for k in range(4):
            mine = jnp.logical_and(y == x, y == k)
            desc = pltpu.make_async_remote_copy(
                src_ref=sums.at[f, 0], dst_ref=sums_in.at[f, k], send_sem=send_sems.at[0],
                recv_sem=sum_sems.at[f, k], device_id=sib, device_id_type=MESH,
            )
            pl.when(jnp.logical_not(mine))(desc.wait_recv)
        total = sums_in[f, 0].astype(F32) + sums_in[f, 1].astype(F32)
        return total + (sums_in[f, 2].astype(F32) + sums_in[f, 3].astype(F32))

    def send_top(f, value):
        top[p, f] = (value + first[f].reshape(256, 256).astype(F32)).astype(BF16)
        block = top.at[p, f]
        return links.start(block, block, across), links.start(block, block, sib)

    def relay_top(f, cross):
        cross.wait_recv()
        block = top.at[across[0], f]
        return links.start(block, block, sib)

    def add_up(f, chunk, fresh):
        rows = top[chunk, f]
        for t in range(4):
            weights = wu[chunk, :, :, t].reshape(256, 256)
            term = jnp.dot(rows, weights, preferred_element_type=F32)
            if fresh:
                up_acc[f, t] = term
            else:
                up_acc[f, t] += term

    def write(f, out):
        for t in range(4):
            for dx in range(2):
                block = up_acc[f, t, :, 128 * dx : 128 * dx + 128].reshape(8, 32, 128)
                spread[t // 2, :, t % 2, pl.ds(dx, 32, stride=2), :] = block
        out[...] = spread[...].astype(BF16)

    to_column(0)
    gc.wait()
    to_sibling(0)
    to_column(1)
    convolve(0, 0)
    convolve(0, 1)
    gu.forward_b(ORDER[0])
    gu.forward_b(ORDER[1])
    to_sibling(1)
    convolve(1, 0)
    value, gain = silu_gain(gather_sums(0))
    keep[...] = gain
    cross_0, near_0 = send_top(0, value)
    gu.forward_b(ORDER[2])
    gu.forward_b(ORDER[3])
    convolve(1, 1)
    relay_0 = relay_top(0, cross_0)
    for g in ORDER:
        gu.wait_b(g)
    add_up(0, p, True)
    cross_1, near_1 = send_top(1, keep[...] * gather_sums(1))
    near_0.wait_recv()
    add_up(0, sib[0], False)
    add_up(0, across[0], False)
    relay_0.wait_recv()
    add_up(0, 2 * (1 - zl) + 1 - c, False)
    write(0, out_s)
    add_up(1, p, True)
    near_1.wait_recv()
    add_up(1, sib[0], False)
    relay_1 = relay_top(1, cross_1)
    add_up(1, across[0], False)
    relay_1.wait_recv()
    add_up(1, 2 * (1 - zl) + 1 - c, False)
    write(1, out_t)
    links.drain()


def local(fine_state, fine_tangent, down_weight, conv_weight, up_weight):
    vmem = pl.BlockSpec(memory_space=pltpu.VMEM)
    fine = (2, 8, 2, 64, 128)
    shape = jax.ShapeDtypeStruct(fine, BF16)
    state, tangent = pl.pallas_call(
        kernel,
        out_shape=(shape, shape),
        in_specs=[vmem] * 5,
        out_specs=(vmem, vmem),
        scratch_shapes=[
            pltpu.VMEM(fine, F32),
            pltpu.VMEM((2, 8, 2, 256, 128), BF16),
            pltpu.VMEM((8, 16, 256), BF16),
            pltpu.VMEM((4, 2, 4, 8, 16, 256), BF16),
            pltpu.VMEM((2, 4, 27, 32, 256), BF16),
            pltpu.VMEM((4, 2, 4, 4, 32, 256), BF16),
            pltpu.VMEM((2, 256, 256), BF16),
            pltpu.VMEM((2, 256, 256), BF16),
            pltpu.VMEM((2, 8, 32, 256), BF16),
            pltpu.VMEM((2, 8, 32, 256), BF16),
            pltpu.VMEM((4, 2, 8, 32, 256), BF16),
            pltpu.VMEM((2, 6, 10, 32, 256), BF16),
            pltpu.VMEM((3, 512, 256), F32),
            pltpu.VMEM((256, 256), F32),
            pltpu.VMEM((2, 4, 256, 256), BF16),
            pltpu.VMEM((2, 4, 256, 256), BF16),
            pltpu.VMEM((4, 2, 256, 256), BF16),
            pltpu.VMEM((2, 4, 256, 256), F32),
            pltpu.VMEM(fine, F32),
            pltpu.SemaphoreType.DMA((LINKS,)),
            pltpu.SemaphoreType.DMA((LINKS,)),
            pltpu.SemaphoreType.DMA((4, 2)),
            pltpu.SemaphoreType.DMA((6, 2)),
            pltpu.SemaphoreType.DMA((2, 4)),
        ],
        compiler_params=pltpu.CompilerParams(
            collective_id=0, has_side_effects=True, vmem_limit_bytes=56 * 2**20
        ),
    )(fine_state.reshape(fine), fine_tangent.reshape(fine), down_weight, conv_weight, up_weight)
    return state.reshape(fine_state.shape), tangent.reshape(fine_state.shape)


def solution(mesh):
    in_specs = (
        P("space", None, None, "param"),
        P("space", None, None, "param"),
        P(None, "space", "param"),
        P(None, "space", "param"),
        P(None, "space", "param"),
    )
    out_specs = (P("space", None, None, "param"), P("space", None, None, "param"))
    return jax.shard_map(local, mesh=mesh, in_specs=in_specs, out_specs=out_specs, check_vma=False)
```

time: 131 us -> 107 us (0.82)
  the two profiles are of different devices: /device:TPU:47 before, /device:TPU:5 now
where the time goes in v3:
time: 107 us; the launch traced here: 106 us
  Pallas kernels  103 us (96%)
  local copies, waits for them, and re-layouts  2.72 us (3%)
    pallas_call x1, Pallas kernels, local(): pl.pallas_call(kernel, out_shape=(shape, shape), in_specs=[vmem] * 5, out...  103 us
    unnamed x4, local copies, waits for them, and re-layouts  2.72 us

profile of v3, /device:TPU:5, one launch (start us, length us, event | category | flops | bytes accessed | tf_op | source)
XLA Modules:
  0.0 106.3 jit_solution(17264173520636226859)
XLA Ops:
  0.6 103.0 %shard_map.68 = (bf16[2,8,2,64,128]{4,3,2,1,0:T(8,128)(2,1)}, bf16[2,8,2,64,128]{4,3,2,1,0:T(8,128)(2,1)}) custom-call(bf16[2,8,2,64,128]{4,3,2,1,0:T(8,128)(2,1)} %bitcast.6, bf16[2,8,2,64,128]{4,3,2,1,0:T(8,128)(2,1)} %bitcast.7, f32[8,16,256]{2,1,0:T(8,128)} %wd32.1, f32[27,32,256]{2,1,0:T(8,128)} %wc32.1, f32[8,32,128]{2,1,0:T(8,128)} %wu32.1), custom_call_target="tpu_custom_call" | custom-call | tf_op jit(solution)/shard_map/pallas_call | solution.py:453
  103.6 0.0 copy-start
  103.6 1.9 %copy.9 = bf16[2,16,64,128]{3,2,1,0:T(8,128)(2,1)} copy(bf16[2,16,64,128]{3,2,1,0:T(8,128)(2,1)} %bitcast.5) | data formatting | bytes 1048576
  105.5 0.0 copy-done
  105.5 0.8 copy.10
Async XLA Ops:
  103.6 1.9 %copy-start = (bf16[2,8,2,64,128]{4,3,2,1,0:T(8,128)(2,1)S(1)}, bf16[2,8,2,64,128]{4,3,2,1,0:T(8,128)(2,1)}, u32[]{:S(2)}) copy-start(bf16[2,8,2,64,128]{4,3,2,1,0:T(8,128)(2,1)} %get-tuple-element.5) | copy-start | bytes 1572868

commit v4 on v3

--- a/solution.py
+++ b/solution.py
@@ -124,7 +124,7 @@
             desc.wait_recv()
 
 
-LINKS = 160
+LINKS = 192
 SPLIT = 6
 ORDER = (0, 1, 3, 2)
 
@@ -132,7 +132,7 @@
 def kernel(
     fs, ft, wd32, wc32, wu32, out_s, out_t,
     ff, taps, wd_own, wd, wc, wu, part, part_in, first, first_z, mid, apad, acc, keep, sums, sums_in,
-    top, up_acc, spread, send_sems, recv_sems, mid_sems, plane_sems, sum_sems,
+    top, up_acc, spread, fine_out, send_sems, recv_sems, mid_sems, plane_sems, sum_sems, out_sems,
 ):
     p = lax.axis_index("param")
     s = lax.axis_index("space")
@@ -238,10 +238,11 @@
 
     part_copy = []
     for f in range(2):
-        part[f] = down(1 - zl, f).astype(BF16)
-        part_copy.append(links.start(part.at[f], part_in.at[f], across))
-    for f in range(2):
-        acc[f, :256] = down(zl, f)
+        for own in range(2):
+            other = down(1 - zl, f) if own == 0 else down(zl, f)
+            acc[f, 256 * (1 - own) : 256 * (2 - own)] = other
+            part[f, own] = other.astype(BF16)
+            part_copy.append(links.start(part.at[f, own], part_in.at[f, own], across))
     gu.after_z()
     apad[:, :, pl.ds(0, 1)] = jnp.zeros((2, 6, 1, 32, 256), BF16)
     apad[:, :, pl.ds(9, 1)] = jnp.zeros((2, 6, 1, 32, 256), BF16)
@@ -268,21 +269,17 @@
         def _():
             mid[y, f] = block[f]
 
-    first_copy = []
     for f in range(2):
-        part_copy[f].wait_recv()
-        pre = acc[f, :256] + part_in[f].astype(F32)
-        if f == 0:
-            value, gain = silu_gain(pre)
-            acc[2, :256] = gain
-        else:
-            value = acc[2, :256] * pre
-        first[f] = value.astype(BF16).reshape(8, 32, 256)
-        first_copy.append(links.start(first.at[f], first_z.at[f], across))
-        to_row(first, p, f)
-    for f in range(2):
-        first_copy[f].wait_recv()
-        to_row(first_z, 2 * (1 - zl) + c, f)
+        for k, block in enumerate((first, first_z)):
+            part_copy[2 * f + k].wait_recv()
+            pre = acc[f, 256 * k : 256 * k + 256] + part_in[f, k].astype(F32)
+            if f == 0:
+                value, gain = silu_gain(pre)
+                acc[2, 256 * k : 256 * k + 256] = gain
+            else:
+                value = acc[2, 256 * k : 256 * k + 256] * pre
+            block[f] = value.astype(BF16).reshape(8, 32, 256)
+            to_row(block, across[0] if k else p, f)
     for g in ORDER:
         gu.start_b(g)
 
@@ -342,12 +339,12 @@
 
     edge = lax.broadcasted_iota(jnp.int32, (1, 32, 1), 1)
 
-    def convolve(f, pair):
+    def convolve(f, h):
         for kx in range(3):
             total = None
             for kz in range(3):
                 for ky in range(3):
-                    rows = apad[f, pl.ds(2 * pair + kz, 2), ky : ky + 8].reshape(512, 256)
+                    rows = apad[f, kz : kz + 4, 4 * h + ky : 4 * h + ky + 4].reshape(512, 256)
                     weights = wc[:, :, 9 * kz + 3 * ky + kx].reshape(256, 256)
                     term = jnp.dot(rows, weights, preferred_element_type=F32)
                     total = term if total is None else total + term
@@ -356,43 +353,45 @@
         high = pltpu.roll(acc[2], 511, 0).reshape(16, 32, 256)
         total = acc[1].reshape(16, 32, 256)
         total = total + jnp.where(edge == 0, 0.0, low) + jnp.where(edge == 31, 0.0, high)
-        sums[f, pl.ds(2 * pair, 2)] = total.reshape(2, 256, 256).astype(BF16)
-        for plane in (2 * pair, 2 * pair + 1):
+        sums[f, h] = total.reshape(4, 128, 256).astype(BF16)
+        for plane in range(4):
             mine = jnp.logical_and(y == x, x == plane)
             away = jnp.logical_not(mine)
             move = links.copy(
-                sums.at[f, plane], sums_in.at[f, y], (p, space(x, zh, plane)), sum_sems.at[f, y]
+                sums.at[f, h, plane], sums_in.at[f, h, y], (p, space(x, zh, plane)),
+                sum_sems.at[2 * f + h, y],
             )
             links.sent.append((away, move))
             pl.when(away)(move.start)
 
             @pl.when(mine)
             def _():
-                sums_in[f, y] = sums[f, plane]
-
-    def gather_sums(f):
+                sums_in[f, h, y] = sums[f, h, plane]
+
+    def gather_sums(f, h):
         for k in range(4):
             mine = jnp.logical_and(y == x, y == k)
             desc = pltpu.make_async_remote_copy(
-                src_ref=sums.at[f, 0], dst_ref=sums_in.at[f, k], send_sem=send_sems.at[0],
-                recv_sem=sum_sems.at[f, k], device_id=sib, device_id_type=MESH,
+                src_ref=sums.at[f, h, 0], dst_ref=sums_in.at[f, h, k], send_sem=send_sems.at[0],
+                recv_sem=sum_sems.at[2 * f + h, k], device_id=sib, device_id_type=MESH,
             )
             pl.when(jnp.logical_not(mine))(desc.wait_recv)
-        total = sums_in[f, 0].astype(F32) + sums_in[f, 1].astype(F32)
-        return total + (sums_in[f, 2].astype(F32) + sums_in[f, 3].astype(F32))
-
-    def send_top(f, value):
-        top[p, f] = (value + first[f].reshape(256, 256).astype(F32)).astype(BF16)
-        block = top.at[p, f]
+        total = sums_in[f, h, 0].astype(F32) + sums_in[f, h, 1].astype(F32)
+        return total + (sums_in[f, h, 2].astype(F32) + sums_in[f, h, 3].astype(F32))
+
+    def send_top(f, h, value):
+        skip = first[f, 4 * h : 4 * h + 4].reshape(128, 256).astype(F32)
+        top[p, f, h] = (value + skip).astype(BF16)
+        block = top.at[p, f, h]
         return links.start(block, block, across), links.start(block, block, sib)
 
-    def relay_top(f, cross):
+    def relay_top(f, h, cross):
         cross.wait_recv()
-        block = top.at[across[0], f]
+        block = top.at[across[0], f, h]
         return links.start(block, block, sib)
 
     def add_up(f, chunk, fresh):
-        rows = top[chunk, f]
+        rows = top[chunk, f].reshape(256, 256)
         for t in range(4):
             weights = wu[chunk, :, :, t].reshape(256, 256)
             term = jnp.dot(rows, weights, preferred_element_type=F32)
@@ -406,8 +405,12 @@
             for dx in range(2):
                 block = up_acc[f, t, :, 128 * dx : 128 * dx + 128].reshape(8, 32, 128)
                 spread[t // 2, :, t % 2, pl.ds(dx, 32, stride=2), :] = block
-        out[...] = spread[...].astype(BF16)
-
+        fine_out[f] = spread[...].astype(BF16)
+        move = pltpu.make_async_copy(fine_out.at[f], out, out_sems.at[f])
+        move.start()
+        return move
+
+    last = 2 * (1 - zl) + 1 - c
     to_column(0)
     gc.wait()
     to_sibling(0)
@@ -418,43 +421,54 @@
     gu.forward_b(ORDER[1])
     to_sibling(1)
     convolve(1, 0)
-    value, gain = silu_gain(gather_sums(0))
-    keep[...] = gain
-    cross_0, near_0 = send_top(0, value)
+    state = []
+    for h in range(2):
+        value, gain = silu_gain(gather_sums(0, h))
+        keep[h] = gain
+        state.append(send_top(0, h, value))
     gu.forward_b(ORDER[2])
     gu.forward_b(ORDER[3])
     convolve(1, 1)
-    relay_0 = relay_top(0, cross_0)
+    relays = [relay_top(0, h, state[h][0]) for h in range(2)]
+    tangent = [send_top(1, 0, keep[0] * gather_sums(1, 0))]
     for g in ORDER:
         gu.wait_b(g)
     add_up(0, p, True)
-    cross_1, near_1 = send_top(1, keep[...] * gather_sums(1))
-    near_0.wait_recv()
+    tangent.append(send_top(1, 1, keep[1] * gather_sums(1, 1)))
+    for h in range(2):
+        state[h][1].wait_recv()
     add_up(0, sib[0], False)
     add_up(0, across[0], False)
-    relay_0.wait_recv()
-    add_up(0, 2 * (1 - zl) + 1 - c, False)
-    write(0, out_s)
+    for h in range(2):
+        relays[h].wait_recv()
+    add_up(0, last, False)
+    relays = [relay_top(1, 0, tangent[0][0])]
+    moves = [write(0, out_s)]
     add_up(1, p, True)
-    near_1.wait_recv()
+    relays.append(relay_top(1, 1, tangent[1][0]))
+    for h in range(2):
+        tangent[h][1].wait_recv()
     add_up(1, sib[0], False)
-    relay_1 = relay_top(1, cross_1)
     add_up(1, across[0], False)
-    relay_1.wait_recv()
-    add_up(1, 2 * (1 - zl) + 1 - c, False)
-    write(1, out_t)
+    for h in range(2):
+        relays[h].wait_recv()
+    add_up(1, last, False)
+    moves.append(write(1, out_t))
+    for move in moves:
+        move.wait()
     links.drain()
 
 
 def local(fine_state, fine_tangent, down_weight, conv_weight, up_weight):
     vmem = pl.BlockSpec(memory_space=pltpu.VMEM)
+    whole = pl.BlockSpec(memory_space=pl.ANY)
     fine = (2, 8, 2, 64, 128)
     shape = jax.ShapeDtypeStruct(fine, BF16)
     state, tangent = pl.pallas_call(
         kernel,
         out_shape=(shape, shape),
         in_specs=[vmem] * 5,
-        out_specs=(vmem, vmem),
+        out_specs=(whole, whole),
         scratch_shapes=[
             pltpu.VMEM(fine, F32),
             pltpu.VMEM((2, 8, 2, 256, 128), BF16),
@@ -462,24 +476,26 @@
             pltpu.VMEM((4, 2, 4, 8, 16, 256), BF16),
             pltpu.VMEM((2, 4, 27, 32, 256), BF16),
             pltpu.VMEM((4, 2, 4, 4, 32, 256), BF16),
-            pltpu.VMEM((2, 256, 256), BF16),
-            pltpu.VMEM((2, 256, 256), BF16),
+            pltpu.VMEM((2, 2, 256, 256), BF16),
+            pltpu.VMEM((2, 2, 256, 256), BF16),
             pltpu.VMEM((2, 8, 32, 256), BF16),
             pltpu.VMEM((2, 8, 32, 256), BF16),
             pltpu.VMEM((4, 2, 8, 32, 256), BF16),
             pltpu.VMEM((2, 6, 10, 32, 256), BF16),
             pltpu.VMEM((3, 512, 256), F32),
-            pltpu.VMEM((256, 256), F32),
-            pltpu.VMEM((2, 4, 256, 256), BF16),
-            pltpu.VMEM((2, 4, 256, 256), BF16),
-            pltpu.VMEM((4, 2, 256, 256), BF16),
+            pltpu.VMEM((2, 128, 256), F32),
+            pltpu.VMEM((2, 2, 4, 128, 256), BF16),
+            pltpu.VMEM((2, 2, 4, 128, 256), BF16),
+            pltpu.VMEM((4, 2, 2, 128, 256), BF16),
             pltpu.VMEM((2, 4, 256, 256), F32),
             pltpu.VMEM(fine, F32),
+            pltpu.VMEM((2,) + fine, BF16),
             pltpu.SemaphoreType.DMA((LINKS,)),
             pltpu.SemaphoreType.DMA((LINKS,)),
             pltpu.SemaphoreType.DMA((4, 2)),
             pltpu.SemaphoreType.DMA((6, 2)),
-            pltpu.SemaphoreType.DMA((2, 4)),
+            pltpu.SemaphoreType.DMA((4, 4)),
+            pltpu.SemaphoreType.DMA((2,)),
         ],
         compiler_params=pltpu.CompilerParams(
             collective_id=0, has_side_effects=True, vmem_limit_bytes=56 * 2**20

time: 107 us -> 101 us (0.944)
  Pallas kernels: 103 us -> 96.7 us
    pallas_call x1, Pallas kernels: 103 us -> 96.7 us  [local(): pl.pallas_call(kernel, out_shape=(shape, shape), in_specs=[vmem] * 5, out...]
where the time goes in v4:
time: 101 us; the launch traced here: 100 us
  Pallas kernels  96.7 us (96%)
  local copies, waits for them, and re-layouts  2.72 us (3%)
    pallas_call x1, Pallas kernels, local(): pl.pallas_call(kernel, out_shape=(shape, shape), in_specs=[vmem] * 5, out...  96.7 us
    unnamed x4, local copies, waits for them, and re-layouts  2.72 us

profile of v4, /device:TPU:5, one launch (start us, length us, event | category | flops | bytes accessed | tf_op | source)
XLA Modules:
  0.0 100.0 jit_solution(18281697065060493890)
XLA Ops:
  0.6 96.7 %shard_map.68 = (bf16[2,8,2,64,128]{4,3,2,1,0:T(8,128)(2,1)}, bf16[2,8,2,64,128]{4,3,2,1,0:T(8,128)(2,1)}) custom-call(bf16[2,8,2,64,128]{4,3,2,1,0:T(8,128)(2,1)} %bitcast.6, bf16[2,8,2,64,128]{4,3,2,1,0:T(8,128)(2,1)} %bitcast.7, f32[8,16,256]{2,1,0:T(8,128)} %wd32.1, f32[27,32,256]{2,1,0:T(8,128)} %wc32.1, f32[8,32,128]{2,1,0:T(8,128)} %wu32.1), custom_call_target="tpu_custom_call" | custom-call | tf_op jit(solution)/shard_map/pallas_call | solution.py:467
  97.3 0.0 copy-start
  97.3 1.9 %copy.9 = bf16[2,16,64,128]{3,2,1,0:T(8,128)(2,1)} copy(bf16[2,16,64,128]{3,2,1,0:T(8,128)(2,1)} %bitcast.5) | data formatting | bytes 1048576
  99.3 0.0 copy-done
  99.3 0.8 copy.10
Async XLA Ops:
  97.3 1.9 %copy-start = (bf16[2,8,2,64,128]{4,3,2,1,0:T(8,128)(2,1)S(1)}, bf16[2,8,2,64,128]{4,3,2,1,0:T(8,128)(2,1)}, u32[]{:S(2)}) copy-start(bf16[2,8,2,64,128]{4,3,2,1,0:T(8,128)(2,1)} %get-tuple-element.5) | copy-start | bytes 1572868

commit v5 on v4

--- a/solution.py
+++ b/solution.py
@@ -125,15 +125,22 @@
 
 
 LINKS = 192
-SPLIT = 6
+SPLIT = 7
 ORDER = (0, 1, 3, 2)
 
 
 def kernel(
-    fs, ft, wd32, wc32, wu32, out_s, out_t,
+    fs, ft, wd32, wc_in, wu_in, out_s, out_t,
+    fine_in, wc32, wu32,
     ff, taps, wd_own, wd, wc, wu, part, part_in, first, first_z, mid, apad, acc, keep, sums, sums_in,
-    top, up_acc, spread, fine_out, send_sems, recv_sems, mid_sems, plane_sems, sum_sems, out_sems,
+    top, up_acc, spread, fine_out, send_sems, recv_sems, mid_sems, plane_sems, sum_sems, out_sems, in_sems,
 ):
+    loads = []
+    for at, (src, dst) in enumerate(
+        ((wc_in, wc32), (fs, fine_in.at[0]), (ft, fine_in.at[1]), (wu_in, wu32))
+    ):
+        loads.append(pltpu.make_async_copy(src, dst, in_sems.at[at]))
+        loads[-1].start()
     p = lax.axis_index("param")
     s = lax.axis_index("space")
     zl, c = p // 2, p % 2
@@ -174,6 +181,7 @@
     moved = links.copy(wd_own, wd.at[(y + 2) % 4, zh, x], swap)
     links.sent.append((jnp.logical_not(placed), moved))
     pl.when(jnp.logical_not(placed))(moved.start)
+    loads[0].wait()
     wc[zh, x] = wc32[...].astype(BF16)
 
     def pick(z):
@@ -194,11 +202,11 @@
         links, lambda z, a, b: wu.at[b, pick(z), a], (zh, x, y),
         devs["zh"], lambda a: (p, space(y, zh, a)), devs["up"], devs["down"],
     )
-    gc.start_z()
     gc.start()
 
-    for f, fine in enumerate((fs, ft)):
-        ff[...] = fine[...].astype(F32)
+    for f in range(2):
+        loads[1 + f].wait()
+        ff[...] = fine_in[f].astype(F32)
         for dz in range(2):
             for dy in range(2):
                 for dx in range(2):
@@ -208,6 +216,8 @@
     pl.when(jnp.logical_not(placed))(moved.wait_recv)
     for part_of in gd:
         part_of.start()
+    gc.start_z()
+    loads[3].wait()
     for t in range(4):
         for dx in range(2):
             wu[y, zh, x, t, :, 128 * dx : 128 * dx + 128] = wu32[2 * t + dx].astype(BF16)
@@ -467,9 +477,12 @@
     state, tangent = pl.pallas_call(
         kernel,
         out_shape=(shape, shape),
-        in_specs=[vmem] * 5,
+        in_specs=[whole, whole, vmem, whole, whole],
         out_specs=(whole, whole),
         scratch_shapes=[
+            pltpu.VMEM((2,) + fine, BF16),
+            pltpu.VMEM(conv_weight.shape, F32),
+            pltpu.VMEM(up_weight.shape, F32),
             pltpu.VMEM(fine, F32),
             pltpu.VMEM((2, 8, 2, 256, 128), BF16),
             pltpu.VMEM((8, 16, 256), BF16),
@@ -496,6 +509,7 @@
             pltpu.SemaphoreType.DMA((6, 2)),
             pltpu.SemaphoreType.DMA((4, 4)),
             pltpu.SemaphoreType.DMA((2,)),
+            pltpu.SemaphoreType.DMA((4,)),
         ],
         compiler_params=pltpu.CompilerParams(
             collective_id=0, has_side_effects=True, vmem_limit_bytes=56 * 2**20

time: 101 us -> 98 us (0.970)
  Pallas kernels: 96.7 us -> 94.5 us
    pallas_call x1, Pallas kernels: 96.7 us -> 94.5 us  [local(): pl.pallas_call(kernel, out_shape=(shape, shape), in_specs=[whole, whole,...]
where the time goes in v5:
time: 98 us; the launch traced here: 97.8 us
  Pallas kernels  94.5 us (96%)
  local copies, waits for them, and re-layouts  2.72 us (3%)
    pallas_call x1, Pallas kernels, local(): pl.pallas_call(kernel, out_shape=(shape, shape), in_specs=[whole, whole,...  94.5 us
    unnamed x4, local copies, waits for them, and re-layouts  2.72 us

profile of v5, /device:TPU:5, one launch (start us, length us, event | category | flops | bytes accessed | tf_op | source)
XLA Modules:
  0.0 97.8 jit_solution(6284293343524813605)
XLA Ops:
  0.6 94.5 %shard_map.68 = (bf16[2,8,2,64,128]{4,3,2,1,0:T(8,128)(2,1)}, bf16[2,8,2,64,128]{4,3,2,1,0:T(8,128)(2,1)}) custom-call(bf16[2,8,2,64,128]{4,3,2,1,0:T(8,128)(2,1)} %bitcast.6, bf16[2,8,2,64,128]{4,3,2,1,0:T(8,128)(2,1)} %bitcast.7, f32[8,16,256]{2,1,0:T(8,128)} %wd32.1, f32[27,32,256]{2,1,0:T(8,128)} %wc_in.1, f32[8,32,128]{2,1,0:T(8,128)} %wu_in.1), custom_call_target="tpu_custom_call" | custom-call | tf_op jit(solution)/shard_map/pallas_call | solution.py:477
  95.1 0.0 copy-start
  95.1 1.9 %copy.9 = bf16[2,16,64,128]{3,2,1,0:T(8,128)(2,1)} copy(bf16[2,16,64,128]{3,2,1,0:T(8,128)(2,1)} %bitcast.5) | data formatting | bytes 1048576
  97.0 0.0 copy-done
  97.0 0.8 copy.10
Async XLA Ops:
  95.1 1.9 %copy-start = (bf16[2,8,2,64,128]{4,3,2,1,0:T(8,128)(2,1)S(1)}, bf16[2,8,2,64,128]{4,3,2,1,0:T(8,128)(2,1)}, u32[]{:S(2)}) copy-start(bf16[2,8,2,64,128]{4,3,2,1,0:T(8,128)(2,1)} %get-tuple-element.5) | copy-start | bytes 1572868

commit v6 on v5

--- a/solution.py
+++ b/solution.py
@@ -422,9 +422,9 @@
 
     last = 2 * (1 - zl) + 1 - c
     to_column(0)
+    to_column(1)
+    to_sibling(0)
     gc.wait()
-    to_sibling(0)
-    to_column(1)
     convolve(0, 0)
     convolve(0, 1)
     gu.forward_b(ORDER[0])

time: 98 us -> 97.2 us (level)
  Pallas kernels: 94.5 us -> 93.2 us
    pallas_call x1, Pallas kernels: 94.5 us -> 93.2 us  [local(): pl.pallas_call(kernel, out_shape=(shape, shape), in_specs=[whole, whole,...]
where the time goes in v6:
time: 97.2 us; the launch traced here: 96.6 us
  Pallas kernels  93.2 us (96%)
  local copies, waits for them, and re-layouts  2.72 us (3%)
    pallas_call x1, Pallas kernels, local(): pl.pallas_call(kernel, out_shape=(shape, shape), in_specs=[whole, whole,...  93.2 us
    unnamed x4, local copies, waits for them, and re-layouts  2.72 us

profile of v6, /device:TPU:5, one launch (start us, length us, event | category | flops | bytes accessed | tf_op | source)
XLA Modules:
  0.0 96.6 jit_solution(3263318926282569558)
XLA Ops:
  0.6 93.2 %shard_map.68 = (bf16[2,8,2,64,128]{4,3,2,1,0:T(8,128)(2,1)}, bf16[2,8,2,64,128]{4,3,2,1,0:T(8,128)(2,1)}) custom-call(bf16[2,8,2,64,128]{4,3,2,1,0:T(8,128)(2,1)} %bitcast.6, bf16[2,8,2,64,128]{4,3,2,1,0:T(8,128)(2,1)} %bitcast.7, f32[8,16,256]{2,1,0:T(8,128)} %wd32.1, f32[27,32,256]{2,1,0:T(8,128)} %wc_in.1, f32[8,32,128]{2,1,0:T(8,128)} %wu_in.1), custom_call_target="tpu_custom_call" | custom-call | tf_op jit(solution)/shard_map/pallas_call | solution.py:477
  93.8 0.0 copy-start
  93.9 1.9 %copy.9 = bf16[2,16,64,128]{3,2,1,0:T(8,128)(2,1)} copy(bf16[2,16,64,128]{3,2,1,0:T(8,128)(2,1)} %bitcast.5) | data formatting | bytes 1048576
  95.8 0.0 copy-done
  95.8 0.8 copy.10
Async XLA Ops:
  93.8 1.9 %copy-start = (bf16[2,8,2,64,128]{4,3,2,1,0:T(8,128)(2,1)S(1)}, bf16[2,8,2,64,128]{4,3,2,1,0:T(8,128)(2,1)}, u32[]{:S(2)}) copy-start(bf16[2,8,2,64,128]{4,3,2,1,0:T(8,128)(2,1)} %get-tuple-element.5) | copy-start | bytes 1572868

commit v7 on v6

--- a/solution.py
+++ b/solution.py
@@ -449,10 +449,11 @@
         state[h][1].wait_recv()
     add_up(0, sib[0], False)
     add_up(0, across[0], False)
+    ahead = relay_top(1, 0, tangent[0][0])
     for h in range(2):
         relays[h].wait_recv()
     add_up(0, last, False)
-    relays = [relay_top(1, 0, tangent[0][0])]
+    relays = [ahead]
     moves = [write(0, out_s)]
     add_up(1, p, True)
     relays.append(relay_top(1, 1, tangent[1][0]))

time: 97.2 us -> 97.2 us (level)
  no operation moved by 1% of the time
where the time goes in v7:
time: 97.2 us; the launch traced here: 96.6 us
  Pallas kernels  93.2 us (96%)
  local copies, waits for them, and re-layouts  2.72 us (3%)
    pallas_call x1, Pallas kernels, local(): pl.pallas_call(kernel, out_shape=(shape, shape), in_specs=[whole, whole,...  93.2 us
    unnamed x4, local copies, waits for them, and re-layouts  2.72 us

profile of v7, /device:TPU:5, one launch (start us, length us, event | category | flops | bytes accessed | tf_op | source)
XLA Modules:
  0.0 96.6 jit_solution(13889261463725240989)
XLA Ops:
  0.6 93.2 %shard_map.68 = (bf16[2,8,2,64,128]{4,3,2,1,0:T(8,128)(2,1)}, bf16[2,8,2,64,128]{4,3,2,1,0:T(8,128)(2,1)}) custom-call(bf16[2,8,2,64,128]{4,3,2,1,0:T(8,128)(2,1)} %bitcast.6, bf16[2,8,2,64,128]{4,3,2,1,0:T(8,128)(2,1)} %bitcast.7, f32[8,16,256]{2,1,0:T(8,128)} %wd32.1, f32[27,32,256]{2,1,0:T(8,128)} %wc_in.1, f32[8,32,128]{2,1,0:T(8,128)} %wu_in.1), custom_call_target="tpu_custom_call" | custom-call | tf_op jit(solution)/shard_map/pallas_call | solution.py:478
  93.8 0.0 copy-start
  93.9 1.9 %copy.9 = bf16[2,16,64,128]{3,2,1,0:T(8,128)(2,1)} copy(bf16[2,16,64,128]{3,2,1,0:T(8,128)(2,1)} %bitcast.5) | data formatting | bytes 1048576
  95.8 0.0 copy-done
  95.8 0.8 copy.10
Async XLA Ops:
  93.8 1.9 %copy-start = (bf16[2,8,2,64,128]{4,3,2,1,0:T(8,128)(2,1)S(1)}, bf16[2,8,2,64,128]{4,3,2,1,0:T(8,128)(2,1)}, u32[]{:S(2)}) copy-start(bf16[2,8,2,64,128]{4,3,2,1,0:T(8,128)(2,1)} %get-tuple-element.5) | copy-start | bytes 1572868
